TPU v7x, 128 devices: a whole 4x4x4 slice. The times are simulated.
128 devices in a mesh: chan: 16 (over z, x_hi, core), seg: 8 (over y, x_lo).
Axes of the slice: x: 4 (x_hi: 2, x_lo: 2; x = x_hi * 2 + x_lo), y: 4, z: 4, core: 2. Of those that a mesh axis runs over, the one named last changes fastest.
Arguments:
- traces: float32 [32, 128, 7680], P('seg', None, 'chan'), may hold values from -40 to 40
- sources: int32 [64], replicated, may hold values from 0 to 127, as said below
- validity: int32 [32, 128], replicated, may hold values from 0 to 1, as said below
Outputs:
- correlation: float32 [64, 128, 512], P('seg', 'chan')
Inputs may be any that keep to these rules, and one draw needn't show every extreme that they name: `sources`: 64 distinct channel indices. `validity`: 1 marks a usable segment of a channel, 0 a discarded one; in every draw some channels are 0 in all segments.
All inputs are finite; a program needn't handle non-finite values.
Results may differ from a plain program's by a relative error of at most 0.0021.
Values may be sent and summed in bfloat16 or wider, within the bound.
A program may use at most 128 MiB of HBM per device.

v0:
```python
import math

import jax
import jax.numpy as jnp
from jax import lax
from jax.sharding import PartitionSpec as P

LAGS = 512


PRECISE = lax.Precision.HIGHEST
EPSILON = 1e-06


def fourier_tables(length):
    inner_len = length // 128
    first_ids = jnp.arange(128, dtype=jnp.int32)
    first_phase = (
        2.0 * math.pi / 128.0 * (first_ids[:, None] * first_ids[None, :] % 128).astype(jnp.float32)
    )
    first_table = jnp.concatenate([jnp.cos(first_phase), -jnp.sin(first_phase)], axis=1)
    inner_ids = jnp.arange(inner_len, dtype=jnp.int32)
    twist_phase = (
        2.0
        * math.pi
        / length
        * (inner_ids[:, None] * first_ids[None, :] % length).astype(jnp.float32)
    )
    half_ids = jnp.arange(inner_len // 2, dtype=jnp.int32)
    second_phase = (
        2.0
        * math.pi
        / inner_len
        * (inner_ids[:, None] * half_ids[None, :] % inner_len).astype(jnp.float32)
    )
    return (
        first_table,
        jnp.cos(twist_phase),
        -jnp.sin(twist_phase),
        jnp.cos(second_phase),
        -jnp.sin(second_phase),
    )


def whiten_rows(rows):
    row_total = rows.shape[0]
    length = rows.shape[1]
    inner_len = length // 128
    first_table, twist_cos, twist_sin, second_cos, second_sin = fourier_tables(length)
    folded = rows.reshape(row_total, 128, inner_len)
    section_one = jnp.einsum("rab,ak->rbk", folded, first_table, precision=PRECISE)
    real_one = section_one[:, :, :128]
    imag_one = section_one[:, :, 128:]
    real_two = real_one * twist_cos - imag_one * twist_sin
    imag_two = real_one * twist_sin + imag_one * twist_cos
    real_out = jnp.einsum("rbk,bm->rmk", real_two, second_cos, precision=PRECISE) - jnp.einsum(
        "rbk,bm->rmk", imag_two, second_sin, precision=PRECISE
    )
    imag_out = jnp.einsum("rbk,bm->rmk", real_two, second_sin, precision=PRECISE) + jnp.einsum(
        "rbk,bm->rmk", imag_two, second_cos, precision=PRECISE
    )
    magnitude = jnp.sqrt(real_out * real_out + imag_out * imag_out)
    level_bins = jnp.mean(magnitude, axis=2, keepdims=True) + EPSILON
    bins_total = real_out.shape[1] * 128
    real_white = (real_out / level_bins).reshape(row_total, bins_total)
    imag_white = (imag_out / level_bins).reshape(row_total, bins_total)
    return jnp.concatenate([real_white, imag_white], axis=1).astype(jnp.bfloat16)


def whiten_segments(segment_rows):
    return lax.map(whiten_rows, segment_rows)


def block_span(bins_total):
    candidates = [candidate for candidate in range(128, 769, 128) if bins_total % candidate == 0]
    return max(candidates)


def lag_tables(first_bin, span_bins, length, lags_count):
    bin_ids = first_bin + jnp.arange(span_bins, dtype=jnp.int32)
    lag_ids = jnp.arange(lags_count, dtype=jnp.int32) - lags_count // 2
    phase_ids = bin_ids[:, None] * lag_ids[None, :] % length
    phases = 2.0 * math.pi / length * phase_ids.astype(jnp.float32)
    weights = jnp.where(bin_ids == 0, 1.0, 2.0).astype(jnp.float32)[:, None]
    return (weights * jnp.cos(phases), weights * jnp.sin(phases))


def correlate_rows(source_white, channel_white, row_count):
    own_channels = channel_white.shape[1]
    bins_total = channel_white.shape[2] // 2
    length = 2 * bins_total
    span_bins = block_span(bins_total)
    running = jnp.zeros((row_count * own_channels, LAGS), jnp.float32)
    for first_bin in range(0, bins_total, span_bins):
        last_bin = first_bin + span_bins
        src_real = source_white[:, :, None, first_bin:last_bin].astype(jnp.float32)
        src_imag = source_white[:, :, None, bins_total + first_bin : bins_total + last_bin].astype(
            jnp.float32
        )
        chan_real = channel_white[:, None, :, first_bin:last_bin].astype(jnp.float32)
        chan_imag = channel_white[
            :, None, :, bins_total + first_bin : bins_total + last_bin
        ].astype(jnp.float32)
        stack_real = jnp.sum(src_real * chan_real + src_imag * chan_imag, axis=0)
        stack_imag = jnp.sum(src_real * chan_imag - src_imag * chan_real, axis=0)
        cos_table, sin_table = lag_tables(first_bin, span_bins, length, LAGS)
        flat_real = stack_real.reshape(row_count * own_channels, span_bins)
        flat_imag = stack_imag.reshape(row_count * own_channels, span_bins)
        running = running + jnp.dot(
            flat_real, cos_table, precision=PRECISE, preferred_element_type=jnp.float32
        )
        running = running - jnp.dot(
            flat_imag, sin_table, precision=PRECISE, preferred_element_type=jnp.float32
        )
    return running.reshape(row_count, own_channels, LAGS)


def local(traces, sources, validity):
    chan_count = lax.axis_size("chan")
    seg_count = lax.axis_size("seg")
    chan_index = lax.axis_index("chan")
    seg_index = lax.axis_index("seg")
    local_segs = traces.shape[0]
    all_channels = traces.shape[1]
    own_channels = all_channels // chan_count
    source_total = sources.shape[0]
    rows_each = source_total // seg_count
    channel_ids = jnp.arange(all_channels, dtype=jnp.int32)
    source_onehot = (sources[:, None] == channel_ids[None, :]).astype(jnp.float32)
    valid_all = validity.astype(jnp.float32)
    source_valid_all = jnp.dot(
        valid_all, source_onehot.T, precision=PRECISE, preferred_element_type=jnp.float32
    )
    valid_local = lax.dynamic_slice_in_dim(valid_all, seg_index * local_segs, local_segs, 0)
    own_valid = lax.dynamic_slice_in_dim(valid_local, chan_index * own_channels, own_channels, 1)
    own_gate = own_valid[:, :, None].astype(jnp.bfloat16)
    channel_white = whiten_segments(
        lax.all_to_all(traces, "chan", split_axis=1, concat_axis=2, tiled=True)
    )
    channel_white = channel_white * own_gate
    own_onehot = lax.dynamic_slice_in_dim(
        source_onehot, chan_index * own_channels, own_channels, 1
    ).astype(jnp.bfloat16)
    placed = jnp.einsum(
        "sc,gcf->gsf", own_onehot, channel_white, preferred_element_type=jnp.float32
    )
    source_white = lax.psum(placed.astype(jnp.bfloat16), "chan")
    summed = lax.psum_scatter(
        correlate_rows(source_white, channel_white, rows_each * lax.axis_size("seg")),
        "seg",
        scatter_dimension=0,
        tiled=True,
    )
    source_columns = lax.dynamic_slice_in_dim(source_valid_all, seg_index * rows_each, rows_each, 1)
    channel_columns = lax.dynamic_slice_in_dim(
        valid_all, chan_index * own_channels, own_channels, 1
    )
    pairs = jnp.dot(
        source_columns.T, channel_columns, precision=PRECISE, preferred_element_type=jnp.float32
    )
    bins_total = channel_white.shape[2] // 2
    return summed / jnp.sqrt(2.0 * bins_total * jnp.maximum(pairs, 1.0))[:, :, None]


def solution(mesh):
    in_specs = (P("seg", None, "chan"), P(), P())
    out_specs = P("seg", "chan", None)
    return jax.shard_map(local, mesh=mesh, in_specs=in_specs, out_specs=out_specs, check_vma=False)
```

profile of v0, /device:TPU:0, one launch (start us, length us, event | category | flops | bytes accessed | tf_op | source)
XLA Modules:
  0.0 366.9 jit_solution(6296399835221511875)
XLA Ops:
  6.5 2.6 copy.15
  9.2 8.1 %all-to-all-start = ((f32[4,128,480]{2,0,1:T(4,128)}), f32[4,128,480]{2,0,1:T(4,128)S(1)}, u32[]{:S(2)}, u32[]{:S(2)}) async-start(f32[4,128,480]{2,0,1:T(4,128)} %copy.15), calls=%async_computation | async-start | bytes 2097152 | tf_op jit(solution)/shard_map/all_to_all | solution.py:138
  17.5 17.8 %all-to-all-done = f32[4,128,480]{2,0,1:T(4,128)S(1)} async-done(((f32[4,128,480]{2,0,1:T(4,128)}), f32[4,128,480]{2,0,1:T(4,128)S(1)}, u32[]{:S(2)}, u32[]{:S(2)}) %all-to-all-start) | async-done | bytes 983072 | tf_op jit(solution)/shard_map/all_to_all | solution.py:138
  36.9 17.2 %while.13 = (s32[]{:T(128)}, bf16[4,8,7680]{2,1,0:T(8,128)(2,1)S(1)}, f32[4,8,7680]{2,1,0:T(8,128)S(1)}, s32[]{:T(128)}) while((s32[]{:T(128)}, bf16[4,8,7680]{2,1,0:T(8,128)(2,1)S(1)}, f32[4,8,7680]{2,1,0:T(8,128)S(1)}, s32[]{:T(128)}) %tuple.68), condition=%wide.region_2.3_spmd, body=%wide.region_0.2_spmd.sunk | while | flops 278931488 | bytes 5979973 | solution.py:71
  42.2 1.1 fusion.297
  46.5 1.1 fusion.297
  54.1 3.1 fusion.57
  57.5 153.1 %all-reduce.2.cloned.1.call-done = bf16[4,64,7680]{2,1,0:T(8,128)(2,1)} async-done(((bf16[4,64,7680]{2,1,0:T(8,128)(2,1)}), bf16[4,64,7680]{2,1,0:T(8,128)(2,1)}) %all-reduce.2.cloned.1.call-update) | async-done | bytes 3932176 | tf_op jit(solution)/shard_map/psum | solution.py:147
  210.7 3.1 slice_convert_fusion.1
  213.8 2.5 add_reduce_fusion.4
  216.3 8.7 %fusion.84 = f32[512,512]{1,0:T(8,128)S(1)} fusion(f32[64,8,768]{2,1,0:T(8,128)S(1)} %get-tuple-element.78, s32[512]{0:T(512)S(1)} %iota_add_fusion.4, f32[768]{0:T(1024)S(1)} %fusion.247), kind=kOutput, calls=%fused_computation.115 | convolution fusion | flops 2419851264 | bytes 2626560 | tf_op jit(solution)/shard_map/dot_general | solution.py:112
  225.0 5.4 %subtract_reduce_fusion.2 = (f32[64,8,768]{2,1,0:T(8,128)S(1)}, f32[64,8,768]{2,1,0:T(8,128)S(1)}, f32[64,8,768]{2,1,0:T(8,128)S(1)}, f32[64,8,768]{2,1,0:T(8,128)S(1)}) fusion(f32[4,8,768]{2,1,0:T(8,128)S(1)} %get-tuple-element.107, f32[4,64,768]{2,1,0:T(8,128)S(1)} %get-tuple-element.97, f32[4,8,768]{2,1,0:T(8,128)S(1)} %get-tuple-element.108, ...), kind=kLoop, calls=%fused_computation.78 | loop fusion | flops 23592960 | bytes 9830400 | tf_op jit(solution)/shard_map/reduce_sum | solution.py:105
  230.4 8.7 %fusion.82 = f32[512,512]{1,0:T(8,128)S(1)} fusion(f32[64,8,768]{2,1,0:T(8,128)S(1)} %get-tuple-element.115, s32[768]{0:T(1024)S(1)} %iota_add_fusion.3, f32[768]{0:T(1024)S(1)} %compare_select_fusion.3, s32[512]{0:T(512)S(1)} %iota_add_fusion.4), kind=kOutput, calls=%fused_computation.113 | convolution fusion | flops 2419851264 | bytes 2629632 | tf_op jit(solution)/shard_map/dot_general | solution.py:109
  239.1 8.9 %fusion.138 = f32[512,512]{1,0:T(8,128)S(1)} fusion(f32[512,512]{1,0:T(8,128)S(1)} %fusion.82, f32[512,512]{1,0:T(8,128)S(1)} %fusion.84, f32[64,8,768]{2,1,0:T(8,128)S(1)} %get-tuple-element.77, s32[512]{0:T(512)S(1)} %iota_add_fusion.4, f32[768]{0:T(1024)S(1)} %fusion.247), kind=kOutput, calls=%fused_computation.160 | convolution fusion | flops 2420375552 | bytes 4723712 | tf_op jit(solution)/shard_map/dot_general | solution.py:109
  248.1 9.0 %fusion.143 = f32[512,512]{1,0:T(8,128)S(1)} fusion(f32[512,512]{1,0:T(8,128)S(1)} %fusion.138, f32[64,8,768]{2,1,0:T(8,128)S(1)} %get-tuple-element.116, s32[768]{0:T(1024)S(1)} %iota_add_fusion.3, f32[768]{0:T(1024)S(1)} %compare_select_fusion.3, s32[512]{0:T(512)S(1)} %iota_add_fusion.4), kind=kOutput, calls=%fused_computation.161 | convolution fusion | flops 2420113408 | bytes 3678208 | tf_op jit(solution)/shard_map/dot_general | solution.py:112
  257.1 8.7 %fusion.148 = f32[512,512]{1,0:T(8,128)S(1)} fusion(f32[512,512]{1,0:T(8,128)S(1)} %fusion.143, f32[64,8,768]{2,1,0:T(8,128)S(1)} %get-tuple-element.74, s32[768]{0:T(1024)S(1)} %iota_add_fusion.2, f32[768]{0:T(1024)S(1)} %compare_select_fusion.2, s32[512]{0:T(512)S(1)} %iota_add_fusion.4), kind=kOutput, calls=%fused_computation.162 | convolution fusion | flops 2420113408 | bytes 3678208 | tf_op jit(solution)/shard_map/dot_general | solution.py:109
  265.8 9.2 %fusion.153 = f32[512,512]{1,0:T(8,128)S(1)} fusion(f32[512,512]{1,0:T(8,128)S(1)} %fusion.148, f32[64,8,768]{2,1,0:T(8,128)S(1)} %get-tuple-element.73, s32[768]{0:T(1024)S(1)} %iota_add_fusion.2, f32[768]{0:T(1024)S(1)} %compare_select_fusion.2, s32[512]{0:T(512)S(1)} %iota_add_fusion.4), kind=kOutput, calls=%fused_computation.163 | convolution fusion | flops 2420113408 | bytes 3678208 | tf_op jit(solution)/shard_map/dot_general | solution.py:112
  275.0 5.2 %subtract_reduce_fusion = (f32[64,8,768]{2,1,0:T(8,128)S(1)}, f32[64,8,768]{2,1,0:T(8,128)S(1)}, f32[64,8,768]{2,1,0:T(8,128)S(1)}, f32[64,8,768]{2,1,0:T(8,128)S(1)}) fusion(f32[4,8,768]{2,1,0:T(8,128)S(1)} %get-tuple-element.104, f32[4,64,768]{2,1,0:T(8,128)S(1)} %get-tuple-element.94, f32[4,8,768]{2,1,0:T(8,128)S(1)} %get-tuple-element.103, ...), kind=kLoop, calls=%fused_computation.74 | loop fusion | flops 23592960 | bytes 9830400 | tf_op jit(solution)/shard_map/reduce_sum | solution.py:105
  280.2 8.8 %fusion.158 = f32[512,512]{1,0:T(8,128)S(1)} fusion(f32[512,512]{1,0:T(8,128)S(1)} %fusion.153, f32[64,8,768]{2,1,0:T(8,128)S(1)} %get-tuple-element.113, s32[768]{0:T(1024)S(1)} %iota_add_fusion.1, f32[768]{0:T(1024)S(1)} %compare_select_fusion.1, s32[512]{0:T(512)S(1)} %iota_add_fusion.4), kind=kOutput, calls=%fused_computation.164 | convolution fusion | flops 2420113408 | bytes 3678208 | tf_op jit(solution)/shard_map/dot_general | solution.py:109
  289.0 9.0 %fusion.163 = f32[512,512]{1,0:T(8,128)S(1)} fusion(f32[512,512]{1,0:T(8,128)S(1)} %fusion.158, f32[64,8,768]{2,1,0:T(8,128)S(1)} %get-tuple-element.114, s32[768]{0:T(1024)S(1)} %iota_add_fusion.1, f32[768]{0:T(1024)S(1)} %compare_select_fusion.1, s32[512]{0:T(512)S(1)} %iota_add_fusion.4), kind=kOutput, calls=%fused_computation.165 | convolution fusion | flops 2420113408 | bytes 3678208 | tf_op jit(solution)/shard_map/dot_general | solution.py:112
  298.0 9.0 %fusion.168 = f32[512,512]{1,0:T(8,128)S(1)} fusion(f32[512,512]{1,0:T(8,128)S(1)} %fusion.163, f32[64,8,768]{2,1,0:T(8,128)S(1)} %get-tuple-element.70, s32[768]{0:T(1024)S(1)} %iota_add_fusion, f32[768]{0:T(1024)S(1)} %compare_select_fusion, s32[512]{0:T(512)S(1)} %iota_add_fusion.4), kind=kOutput, calls=%fused_computation.166 | convolution fusion | flops 2420113408 | bytes 3678208 | tf_op jit(solution)/shard_map/dot_general | solution.py:109
  307.0 9.8 %fusion.178 = f32[64,8,512]{2,1,0:T(8,128)} fusion(f32[512,512]{1,0:T(8,128)S(1)} %fusion.168, f32[64,8,768]{2,1,0:T(8,128)S(1)} %get-tuple-element.69, s32[768]{0:T(1024)S(1)} %iota_add_fusion, f32[768]{0:T(1024)S(1)} %compare_select_fusion, s32[512]{0:T(512)S(1)} %iota_add_fusion.4), kind=kOutput, calls=%fused_computation.168 | convolution fusion | flops 2420113408 | bytes 3678208 | tf_op jit(solution)/shard_map/dot_general | solution.py:112
  317.2 40.8 %reduce-scatter.2.cloned.1.call-done = f32[8,8,512]{2,1,0:T(8,128)} async-done(((f32[64,8,512]{2,1,0:T(8,128)}), f32[8,8,512]{2,1,0:T(8,128)}) %reduce-scatter.2.cloned.1.call-update) | async-done | bytes 131088 | tf_op jit(solution)/shard_map/reduce_scatter | solution.py:148
  358.0 1.6 broadcast_divide_fusion
  (83 shorter events, 17.0 us)
Async XLA Ops:
  6.5 10.8 %copy-start = (s32[32,128]{1,0:T(8,128)S(1)}, s32[32,128]{1,0:T(8,128)}, u32[]{:S(2)}) copy-start(s32[32,128]{1,0:T(8,128)} %param.7) | copy-start | bytes 49156
  9.2 8.3 %copy-start.1 = (s32[64]{0:T(128)S(1)}, s32[64]{0:T(128)}, u32[]{:S(2)}) copy-start(s32[64]{0:T(128)} %param.6) | copy-start | bytes 772
  9.2 26.1 %all-to-all-start = ((f32[4,128,480]{2,0,1:T(4,128)}), f32[4,128,480]{2,0,1:T(4,128)S(1)}, u32[]{:S(2)}, u32[]{:S(2)}) async-start(f32[4,128,480]{2,0,1:T(4,128)} %copy.15), calls=%async_computation | async-start | bytes 2097152 | tf_op jit(solution)/shard_map/all_to_all | solution.py:138
  17.3 193.4 %all-reduce.2.cloned.1.call-start = ((), (), s32[]{:S(2)}) async-start(), calls=%async_computation.2 | async-start | bytes 7864320 | tf_op jit(solution)/shard_map/psum | solution.py:147
  57.3 300.7 %reduce-scatter.2.cloned.1.call-start = ((), (), s32[]{:S(2)}) async-start(), calls=%async_computation.3 | async-start | bytes 1179648 | tf_op jit(solution)/shard_map/reduce_scatter | solution.py:148
Sparse Core Ops, SparseCore 0:
  57.4 153.2 all-reduce.1
  316.9 41.0 reduce-scatter.1
where the time goes:
time: 373 us; the launch traced here: 367 us
  waiting for transfers between devices  212 us (57%)
  matrix products  104 us (28%)
  other arithmetic  20.3 us (5%)
  between operations  14.1 us (4%)
  starting transfers between devices  8.2 us (2%)
  local copies, waits for them, and re-layouts  7.91 us (2%)
    psum x1, waiting for transfers between devices, local(): source_white = lax.psum(placed.astype(jnp.bfloat16), 'chan')  153 us
    dot_general x5, matrix products, correlate_rows(): jnp.dot(flat_imag, sin_table, precision=PRECISE, preferred_element_type=j...  45.7 us
    dot_general x5, matrix products, correlate_rows(): jnp.dot(flat_real, cos_table, precision=PRECISE, preferred_element_type=j...  44.1 us
    reduce_scatter x1, waiting for transfers between devices, local(): lax.psum_scatter(correlate_rows(source_white, channel_white, rows_each *...  40.8 us
    all_to_all x1, waiting for transfers between devices, local(): lax.all_to_all(traces, 'chan', split_axis=1, concat_axis=2, tiled=True)  17.8 us
    reduce_sum x2, other arithmetic, correlate_rows(): stack_imag = jnp.sum(src_real * chan_imag - src_imag * chan_real, axis=0)  10.6 us
    all_to_all x1, starting transfers between devices, local(): lax.all_to_all(traces, 'chan', split_axis=1, concat_axis=2, tiled=True)  8.12 us
  transfers between devices with their start and end apart: 3, of which 3 were waited for; matrix products, arithmetic and copies ran while one was open for 0% of the time, Pallas kernels for 0%

commit v1 on v0

v1 whole, which is shorter than its diff:
```python
import functools
import math

import jax
import jax.numpy as jnp
import numpy as np
from jax import lax
from jax.experimental import pallas as pl
from jax.experimental.pallas import tpu as pltpu
from jax.sharding import PartitionSpec as P

LAGS = 512
EPSILON = 1e-06
MESH = pl.DeviceIdType.MESH
CHUNKS = 4
F32 = jnp.float32
BF16 = jnp.bfloat16


def constant_tables(length, blocks):
    block_len = length // blocks
    half = block_len // 2
    q = np.arange(block_len)[:, None]
    k1 = np.arange(blocks)[:, None]
    k2 = np.arange(half)[None, :]
    angle = 2.0 * math.pi / length * ((k1 * q.T) % length)
    twist = np.zeros((2, blocks, 512), np.float32)
    twist[0, :, :block_len] = np.cos(angle)
    twist[1, :, :block_len] = np.sin(angle)
    angle = 2.0 * math.pi / block_len * ((q * k2) % block_len)
    second = np.zeros((2, 512, 256), np.float32)
    second[0, :block_len, :half] = np.cos(angle)
    second[1, :block_len, :half] = np.sin(angle)
    second_hi = second.astype(jnp.bfloat16)
    second_lo = (second - second_hi.astype(np.float32)).astype(jnp.bfloat16)
    lag = (np.arange(LAGS) - LAGS // 2)[None, :]
    angle = 2.0 * math.pi / length * ((k1 * lag) % length)
    lag_one = np.stack([np.cos(angle), np.sin(angle)]).astype(np.float32)
    angle = 2.0 * math.pi / block_len * ((k2.T * lag) % block_len)
    lag_two = np.zeros((2, 256, LAGS), np.float32)
    lag_two[0, :half] = 2.0 * np.cos(angle)
    lag_two[1, :half] = 2.0 * np.sin(angle)
    return twist, second_hi, second_lo, lag_one, lag_two


def times_root(value, k, n):
    re, im = value
    c, s = math.cos(2.0 * math.pi * k / n), math.sin(2.0 * math.pi * k / n)
    if k == 0:
        return value
    if 4 * k == n:
        return (im, -re)
    if 2 * k == n:
        return (-re, None if im is None else -im)
    if im is None:
        return (re * c, re * (-s))
    return (re * c + im * s, im * c - re * s)


def plus(a, b):
    if a is None:
        return b
    return a if b is None else a + b


def conj(value):
    re, im = value
    return (re, None if im is None else -im)


def real_dft(xs):
    n = len(xs)
    if n == 2:
        return [(xs[0] + xs[1], None), (xs[0] - xs[1], None)]
    even, odd = real_dft(xs[0::2]), real_dft(xs[1::2])
    h = n // 2
    out = []
    for k in range(h + 1):
        i = k % h
        e = even[i] if i <= h // 2 else conj(even[h - i])
        o = odd[i] if i <= h // 2 else conj(odd[h - i])
        t = times_root(o, k, n)
        out.append((plus(e[0], t[0]), plus(e[1], t[1])))
    return out


def split(value):
    hi = value.astype(BF16)
    return hi, (value - hi.astype(F32)).astype(BF16)


def dot(a, b):
    return jnp.dot(a, b, preferred_element_type=F32)


def body(
    sources,
    traces,
    validity,
    twist,
    second_hi,
    second_lo,
    lag_one,
    lag_two,
    out,
    src_send,
    own_recv,
    src_recv,
    h_hi,
    h_lo,
    table_hi,
    table_lo,
    spec,
    own_white,
    gathered,
    lag_table,
    prod,
    acc,
    part_recv,
    own_ss,
    own_rs,
    src_ss,
    src_rs,
    ag_ss,
    ag_rs,
    fw_ss,
    fw_rs,
    rs_ss,
    rs_rs,
):
    chans = lax.axis_size("chan")
    segs = lax.axis_size("seg")
    chips = chans // 2
    me = lax.axis_index("chan")
    seg = lax.axis_index("seg")
    chip = me // 2
    core = me % 2
    block_len = traces.shape[2]

    barrier = pltpu.get_barrier_semaphore()
    for d in range(1, chans):
        pl.semaphore_signal(
            barrier, inc=1, device_id=((me + d) % chans, seg), device_id_type=MESH
        )
    for d in range(1, segs):
        pl.semaphore_signal(
            barrier, inc=1, device_id=(me, (seg + d) % segs), device_id_type=MESH
        )

    def pick(s, carry):
        src_send[:, pl.ds(s, 1), :] = traces[:, pl.ds(sources[s], 1), :]
        return carry

    lax.fori_loop(0, 8 * chips, pick, 0)
    pl.semaphore_wait(barrier, chans - 1 + segs - 1)

    src_copies, own_copies = [], []
    for d in range(1, chans):
        to = (me + d) % chans
        copy = pltpu.make_async_remote_copy(
            src_ref=src_send.at[pl.ds(2 * (to % 2), 2), pl.ds(8 * (to // 2), 8)],
            dst_ref=src_recv.at[me],
            send_sem=src_ss.at[d],
            recv_sem=src_rs.at[d],
            device_id=(to, seg),
            device_id_type=MESH,
        )
        copy.start()
        src_copies.append(copy)
    for d in range(1, chans):
        to = (me + d) % chans
        copy = pltpu.make_async_remote_copy(
            src_ref=traces.at[:, pl.ds(8 * to, 8)],
            dst_ref=own_recv.at[me],
            send_sem=own_ss.at[d],
            recv_sem=own_rs.at[d],
            device_id=(to, seg),
            device_id_type=MESH,
        )
        copy.start()
        own_copies.append(copy)
    src_recv[pl.ds(me, 1)] = src_send[
        pl.ds(2 * core, 2), pl.ds(pl.multiple_of(8 * chip, 8), 8), :
    ][None]
    own_recv[pl.ds(me, 1)] = traces[:, pl.ds(pl.multiple_of(8 * me, 8), 8), :][None]

    table_hi[:512, :256] = second_hi[0]
    table_hi[512:, :256] = second_hi[1]
    table_hi[:512, 256:] = -second_hi[1]
    table_hi[512:, 256:] = second_hi[0]
    table_lo[:512, :256] = second_lo[0]
    table_lo[512:, :256] = second_lo[1]
    table_lo[:512, 256:] = -second_lo[1]
    table_lo[512:, 256:] = second_lo[0]

    def fill(k1, carry):
        c1 = lag_one[0, pl.ds(k1, 1), :]
        s1 = lag_one[1, pl.ds(k1, 1), :]

        def rows(i, inner):
            r = pl.multiple_of(i * 16, 16)
            c2 = lag_two[0, pl.ds(r, 16), :]
            s2 = lag_two[1, pl.ds(r, 16), :]
            lag_table[k1, pl.ds(r, 16), :] = (c1 * c2 - s1 * s2).astype(BF16)
            lag_table[k1, pl.ds(r + 256, 16), :] = (-(s1 * c2 + c1 * s2)).astype(BF16)
            return inner

        return lax.fori_loop(0, 16, rows, carry)

    lax.fori_loop(0, chans, fill, 0)
    first = lax.broadcasted_iota(jnp.int32, (16, LAGS), 0) == 0
    head = lag_table[0, :16, :].astype(F32)
    lag_table[0, :16, :] = jnp.where(first, 0.5 * head, head).astype(BF16)

    valid = validity[...].astype(F32).astype(BF16)
    all_segs, all_chans = valid.shape

    def iota(shape, axis):
        return lax.broadcasted_iota(jnp.int32, shape, axis)

    def gate_of(row_seg, row_chan, rows):
        seg_hot = (iota((rows, all_segs), 1) == row_seg).astype(F32).astype(BF16)
        chan_hot = (iota((rows, all_chans), 1) == row_chan).astype(F32)
        return jnp.sum(dot(seg_hot, valid) * chan_hot, axis=1, keepdims=True)

    r32 = iota((32, 1), 0)
    own_gate = gate_of(4 * seg + r32 // 8, 8 * me + r32 % 8, 32)
    r16 = iota((16, 1), 0)
    names = jnp.zeros((16, 1), jnp.int32)
    for s in range(8):
        names = jnp.where(r16 % 8 == s, sources[8 * chip + s], names)
    src_gate = gate_of(4 * seg + 2 * core + r16 // 8, names, 16)
    names = jnp.zeros((8, 1), jnp.int32)
    r8 = iota((8, 1), 0)
    for s in range(8):
        names = jnp.where(r8 == s, sources[8 * seg + s], names)
    want = (iota((8, all_chans), 1) == names).astype(F32).astype(BF16)
    want_valid = lax.dot_general(
        want, valid, (((1,), (1,)), ((), ())), preferred_element_type=F32
    ).astype(BF16)
    pairs_all = dot(want_valid, valid)
    shift_hot = (iota((all_chans, 128), 0) == 8 * me + iota((all_chans, 128), 1)).astype(F32)
    pairs = dot(pairs_all.astype(BF16), shift_hot.astype(BF16))
    bins_total = chans * block_len // 2
    scale = 1.0 / jnp.sqrt(2.0 * bins_total * jnp.maximum(pairs, 1.0))

    spread = (
        (iota((256, 256), 0) // 8 == iota((256, 256), 1) // 8).astype(F32).astype(BF16)
    )

    pad = jnp.zeros((h_hi.shape[1], 128), BF16)
    for k in range(chans):
        h_hi[k, :, 384:512] = pad
        h_hi[k, :, 896:1024] = pad
        h_lo[k, :, 384:512] = pad
        h_lo[k, :, 896:1024] = pad

    tiles = [(a, min(a + 128, block_len)) for a in range(0, block_len, 128)]

    def transform(recv, rows, gate, store):
        def sixteen(i, carry):
            r = pl.multiple_of(i * 16, 16)
            for a, b in tiles:
                xs = [
                    recv[p, pl.ds(2 * i, 2), :, a:b].reshape(16, b - a) for p in range(chans)
                ]
                half = real_dft(xs)
                for k in range(chans):
                    g = half[k] if k <= chans // 2 else conj(half[chans - k])
                    re, im = g
                    if k > 0:
                        c = twist[0, k : k + 1, a:b]
                        s = twist[1, k : k + 1, a:b]
                        if im is None:
                            re, im = re * c, -(re * s)
                        else:
                            re, im = re * c + im * s, im * c - re * s
                    elif im is None:
                        im = jnp.zeros_like(re)
                    hi, lo = split(re)
                    h_hi[k, pl.ds(r, 16), a:b] = hi
                    h_lo[k, pl.ds(r, 16), a:b] = lo
                    hi, lo = split(im)
                    h_hi[k, pl.ds(r, 16), 512 + a : 512 + b] = hi
                    h_lo[k, pl.ds(r, 16), 512 + a : 512 + b] = lo
            return carry

        lax.fori_loop(0, rows // 16, sixteen, 0)

        def second(k, total):
            hi = h_hi[k, :rows, :]
            lo = h_lo[k, :rows, :]
            x = dot(hi, table_hi[...]) + dot(lo, table_hi[...]) + dot(hi, table_lo[...])
            spec[k, :rows, :] = x
            re, im = x[:, :256], x[:, 256:]
            return total + jnp.sqrt(re * re + im * im)

        total = lax.fori_loop(0, chans, second, jnp.zeros((rows, 256), F32))
        hi, lo = split(total)
        level = (dot(hi, spread) + dot(lo, spread)) * (1.0 / 128.0) + EPSILON
        factor = gate / level

        def whiten(k, carry):
            store(k, spec[k, :rows, :256] * factor, spec[k, :rows, 256:] * factor)
            return carry

        lax.fori_loop(0, chans, whiten, 0)

    def store_src(k, re, im):
        gathered[me, k, :, :256] = re.astype(BF16)
        gathered[me, k, :, 256:] = im.astype(BF16)

    def store_own(k, re, im):
        own_white[k, :, :256] = re.astype(BF16).astype(F32)
        own_white[k, :, 256:] = im.astype(BF16).astype(F32)

    for copy in src_copies:
        copy.wait_recv()
    transform(src_recv, 16, src_gate, store_src)

    per = chans // CHUNKS
    partner = (2 * chip + 1 - core, seg)
    ag_copies = [[] for _ in range(CHUNKS)]
    fw_copies = [[] for _ in range(CHUNKS)]
    for ch in range(CHUNKS):
        for d in range(1, chips):
            ref = gathered.at[me, pl.ds(ch * per, per)]
            copy = pltpu.make_async_remote_copy(
                src_ref=ref,
                dst_ref=ref,
                send_sem=ag_ss.at[ch, d],
                recv_sem=ag_rs.at[ch, d],
                device_id=((me + 2 * d) % chans, seg),
                device_id_type=MESH,
            )
            copy.start()
            ag_copies[ch].append(copy)

    def forward(ch, d):
        slot = (me + chans - 2 * d) % chans
        ref = gathered.at[slot, pl.ds(ch * per, per)]
        copy = pltpu.make_async_remote_copy(
            src_ref=ref,
            dst_ref=ref,
            send_sem=fw_ss.at[ch, d],
            recv_sem=fw_rs.at[ch, d],
            device_id=partner,
            device_id_type=MESH,
        )
        copy.start()
        fw_copies[ch].append(copy)

    for ch in range(CHUNKS):
        forward(ch, 0)

    for copy in own_copies:
        copy.wait_recv()
    transform(own_recv, 32, own_gate, store_own)

    acc[...] = jnp.zeros_like(acc)

    def stack(k, carry):
        def octet(o, inner):
            base = pl.multiple_of(o * 64, 64)
            for l in range(2):
                re_at, im_at = l * 128, 256 + l * 128
                ar, ai = [], []
                for h in range(2):
                    re = gathered[2 * o + h, k, :, re_at : re_at + 128].astype(F32)
                    im = gathered[2 * o + h, k, :, im_at : im_at + 128].astype(F32)
                    ar += [re[:8], re[8:]]
                    ai += [im[:8], im[8:]]
                for c in range(0, 8, 2):
                    res, ims = [], []
                    for cc in (c, c + 1):
                        re = im = None
                        for g in range(4):
                            row = 8 * g + cc
                            br = own_white[k, row : row + 1, re_at : re_at + 128]
                            bi = own_white[k, row : row + 1, im_at : im_at + 128]
                            re = plus(re, ar[g] * br + ai[g] * bi)
                            im = plus(im, ar[g] * bi - ai[g] * br)
                        res.append(re)
                        ims.append(im)
                    at = pl.ds(base + 8 * c, 16)
                    prod[at, re_at : re_at + 128] = jnp.concatenate(res, 0).astype(BF16)
                    prod[at, im_at : im_at + 128] = jnp.concatenate(ims, 0).astype(BF16)
            return inner

        lax.fori_loop(0, chips, octet, 0)
        acc[...] += dot(prod[...], lag_table[k])
        return carry

    for ch in range(CHUNKS):
        for d in range(1, chips):
            ag_copies[ch][d - 1].wait_recv()
            forward(ch, d)
        for copy in fw_copies[ch]:
            copy.wait_recv()
        lax.fori_loop(ch * per, (ch + 1) * per, stack, 0)

    rs_copies = []
    for d in range(1, segs):
        to = (seg + d) % segs
        copy = pltpu.make_async_remote_copy(
            src_ref=acc.at[pl.ds(64 * to, 64)],
            dst_ref=part_recv.at[d],
            send_sem=rs_ss.at[d],
            recv_sem=rs_rs.at[d],
            device_id=(me, to),
            device_id_type=MESH,
        )
        copy.start()
        rs_copies.append(copy)
    for copy in rs_copies:
        copy.wait_recv()
    for c in range(8):
        total = acc[pl.ds(pl.multiple_of(64 * seg, 64) + 8 * c, 8), :]
        for d in range(1, segs):
            total += part_recv[d, 8 * c : 8 * c + 8, :]
        out[:, c, :] = total * scale[:, c : c + 1]

    for copy in src_copies + own_copies + rs_copies:
        copy.wait_send()
    for ch in range(CHUNKS):
        for copy in ag_copies[ch] + fw_copies[ch]:
            copy.wait_send()


def local(tables, traces, sources, validity):
    chans = lax.axis_size("chan")
    segs = lax.axis_size("seg")
    vmem = pl.BlockSpec(memory_space=pltpu.VMEM)
    block_len = traces.shape[2]
    dma = pltpu.SemaphoreType.DMA
    return pl.pallas_call(
        body,
        name="correlate",
        out_shape=jax.ShapeDtypeStruct((8, 8, LAGS), F32),
        in_specs=[pl.BlockSpec(memory_space=pltpu.SMEM)] + [vmem] * 7,
        out_specs=vmem,
        scratch_shapes=[
            pltpu.VMEM((4, 64, block_len), F32),
            pltpu.VMEM((chans, 4, 8, block_len), F32),
            pltpu.VMEM((chans, 2, 8, block_len), F32),
            pltpu.VMEM((chans, 32, 1024), BF16),
            pltpu.VMEM((chans, 32, 1024), BF16),
            pltpu.VMEM((1024, 512), BF16),
            pltpu.VMEM((1024, 512), BF16),
            pltpu.VMEM((chans, 32, 512), F32),
            pltpu.VMEM((chans, 32, 512), F32),
            pltpu.VMEM((chans, chans, 16, 512), BF16),
            pltpu.VMEM((chans, 512, LAGS), BF16),
            pltpu.VMEM((512, 512), BF16),
            pltpu.VMEM((512, LAGS), F32),
            pltpu.VMEM((segs, 64, LAGS), F32),
            dma((chans,)),
            dma((chans,)),
            dma((chans,)),
            dma((chans,)),
            dma((CHUNKS, chans // 2)),
            dma((CHUNKS, chans // 2)),
            dma((CHUNKS, chans // 2)),
            dma((CHUNKS, chans // 2)),
            dma((segs,)),
            dma((segs,)),
        ],
        compiler_params=pltpu.CompilerParams(
            collective_id=0, has_side_effects=True, vmem_limit_bytes=60 * 1024 * 1024
        ),
    )(sources, traces, validity, *[jnp.asarray(t) for t in tables])


def solution(mesh):
    chans = mesh.shape["chan"]
    length = 7680
    tables = constant_tables(length, chans)
    return jax.shard_map(
        functools.partial(local, tables),
        mesh=mesh,
        in_specs=(P("seg", None, "chan"), P(), P()),
        out_specs=P("seg", "chan", None),
        check_vma=False,
    )
```

time: 373 us -> 86.1 us (0.23)
  the two profiles are of different devices: /device:TPU:0 before, /device:TPU:1 now
where the time goes in v1:
time: 86.1 us; the launch traced here: 85.9 us
  Pallas kernels  81.8 us (95%)
  local copies, waits for them, and re-layouts  4.1 us (5%)
    pallas_call x1, Pallas kernels, local(): pl.pallas_call(body, name='correlate', out_shape=jax.ShapeDtypeStruct((8,...  81.8 us
    unnamed x2, local copies, waits for them, and re-layouts  4.1 us

profile of v1, /device:TPU:1, one launch (start us, length us, event | category | flops | bytes accessed | tf_op | source)
XLA Modules:
  0.0 85.9 jit_solution(11832425368950628711)
XLA Ops:
  0.0 2.5 %copy.9.traces = f32[4,128,480]{2,1,0:T(8,128)} copy(f32[4,128,480]{1,2,0:T(8,128)} %param.8) | data formatting | bytes 1966080 | tf_op args[0]
  2.5 81.8 %correlate.1 = f32[8,8,512]{2,1,0:T(8,128)} custom-call(s32[64]{0:T(128)} %sources.1, f32[4,128,480]{2,1,0:T(8,128)} %copy.9.traces, s32[32,128]{1,0:T(8,128)} %validity.1, f32[2,16,512]{2,1,0:T(8,128)} %constant.10.clone.twist, bf16[2,512,256]{2,1,0:T(8,128)(2,1)} %constant.11.clone.second_hi, bf16[2,512,256]{2,1,0:T(8,128)(2,1)} %constant.12.clone.second_lo, ...), custom_call_target="tpu_custom_call" | custom-call | tf_op jit(solution)/shard_map/correlate/pallas_call | solution.py:436
  84.4 1.6 %copy.11 = f32[8,8,512]{2,1,0:T(8,128)} copy(f32[8,8,512]{2,1,0:T(8,128)} %correlate.1) | data formatting | bytes 262144

commit v2 on v1

v2 whole, which is shorter than its diff:
```python
import functools
import math

import jax
import jax.numpy as jnp
import numpy as np
from jax import lax
from jax.experimental import pallas as pl
from jax.experimental.pallas import tpu as pltpu
from jax.sharding import PartitionSpec as P

LAGS = 512
EPSILON = 1e-06
MESH = pl.DeviceIdType.MESH
CHUNKS = 8
X_FIRST = (1, 4, 7)
STEPS = 32000.0
F32 = jnp.float32
BF16 = jnp.bfloat16


def constant_tables(length, blocks):
    block_len = length // blocks
    half = block_len // 2
    q = np.arange(block_len)[:, None]
    k1 = np.arange(blocks)[:, None]
    k2 = np.arange(half)[None, :]
    angle = 2.0 * math.pi / length * ((k1 * q.T) % length)
    twist = np.zeros((2, blocks, 512), np.float32)
    twist[0, :, :block_len] = np.cos(angle)
    twist[1, :, :block_len] = np.sin(angle)
    angle = 2.0 * math.pi / block_len * ((q * k2) % block_len)
    second = np.zeros((2, 512, 256), np.float32)
    second[0, :block_len, :half] = np.cos(angle)
    second[1, :block_len, :half] = np.sin(angle)
    second_hi = second.astype(jnp.bfloat16)
    second_lo = (second - second_hi.astype(np.float32)).astype(jnp.bfloat16)
    lag = (np.arange(LAGS) - LAGS // 2)[None, :]
    angle = 2.0 * math.pi / length * ((k1 * lag) % length)
    lag_one = np.stack([np.cos(angle), np.sin(angle)]).astype(np.float32)
    angle = 2.0 * math.pi / block_len * ((k2.T * lag) % block_len)
    lag_two = np.zeros((2, 256, LAGS), np.float32)
    lag_two[0, :half] = 2.0 * np.cos(angle)
    lag_two[1, :half] = 2.0 * np.sin(angle)
    return twist, second_hi, second_lo, lag_one, lag_two


def times_root(value, k, n):
    re, im = value
    c, s = math.cos(2.0 * math.pi * k / n), math.sin(2.0 * math.pi * k / n)
    if k == 0:
        return value
    if 4 * k == n:
        return (im, -re)
    if 2 * k == n:
        return (-re, None if im is None else -im)
    if im is None:
        return (re * c, re * (-s))
    return (re * c + im * s, im * c - re * s)


def plus(a, b):
    if a is None:
        return b
    return a if b is None else a + b


def conj(value):
    re, im = value
    return (re, None if im is None else -im)


def real_dft(xs):
    n = len(xs)
    if n == 2:
        return [(xs[0] + xs[1], None), (xs[0] - xs[1], None)]
    even, odd = real_dft(xs[0::2]), real_dft(xs[1::2])
    h = n // 2
    out = []
    for k in range(h + 1):
        i = k % h
        e = even[i] if i <= h // 2 else conj(even[h - i])
        o = odd[i] if i <= h // 2 else conj(odd[h - i])
        t = times_root(o, k, n)
        out.append((plus(e[0], t[0]), plus(e[1], t[1])))
    return out


def split(value):
    hi = value.astype(BF16)
    return hi, (value - hi.astype(F32)).astype(BF16)


def dot(a, b):
    return jnp.dot(a, b, preferred_element_type=F32)


def body(
    sources,
    traces,
    validity,
    twist,
    second_hi,
    second_lo,
    lag_one,
    lag_two,
    out,
    own_send,
    src_send,
    own_recv,
    src_recv,
    h_hi,
    h_lo,
    table_hi,
    table_lo,
    spec,
    white,
    mine,
    gathered,
    lag_table,
    prod_a,
    prod_b,
    acc,
    part_send,
    part_recv,
    own_ss,
    own_rs,
    src_ss,
    src_rs,
    ag_ss,
    fw_ss,
    ag_rs,
    wh_sem,
    rs_ss,
    rs_rs,
):
    chans = lax.axis_size("chan")
    segs = lax.axis_size("seg")
    me = lax.axis_index("chan")
    seg = lax.axis_index("seg")
    chip = me // 2
    core = me % 2
    z = chip // 2
    plane = chip % 2
    zs = chans // 4
    block_len = traces.shape[1]
    partner = (2 * chip + 1 - core, seg)

    def iota(shape, axis):
        return lax.broadcasted_iota(jnp.int32, shape, axis)

    def remote(src, dst, send, recv, to):
        return pltpu.make_async_remote_copy(
            src_ref=src,
            dst_ref=dst,
            send_sem=send,
            recv_sem=recv,
            device_id=to,
            device_id_type=MESH,
        )

    def device(zz, pp, cc):
        return ((zz % zs) * 4 + pp * 2 + cc, seg)

    barrier = pltpu.get_barrier_semaphore()
    for d in range(1, chans):
        pl.semaphore_signal(
            barrier, inc=1, device_id=((me + d) % chans, seg), device_id_type=MESH
        )
    for d in range(1, segs):
        for c in range(2):
            pl.semaphore_signal(
                barrier,
                inc=1,
                device_id=(2 * chip + c, (seg + d) % segs),
                device_id_type=MESH,
            )

    all_chans = traces.shape[2]
    count = 8 * chans // 2
    names = jnp.zeros((count, 1), jnp.int32)
    r_names = iota((count, 1), 0)
    for s in range(count):
        names = jnp.where(r_names == s, sources[s], names)
    row = iota((all_chans, 1), 0)
    pick = jnp.concatenate([row, names], 0)
    pick = (iota((all_chans + count, all_chans), 1) == pick).astype(F32).astype(BF16)

    def steps_of(g):
        x = traces[g]
        top = jnp.maximum(jnp.max(jnp.abs(x), axis=0, keepdims=True), 1e-30)
        power = jnp.ceil(jnp.log(top) * (128.0 / math.log(2.0))) + 1.0
        steps = jnp.round(x * (STEPS / jnp.exp2(power * (1.0 / 128.0))))
        tail = jnp.where(iota((512 - block_len, all_chans), 0) == 0, power, 0.0)
        steps = jnp.concatenate([steps, tail], 0)
        high = jnp.round(steps * (1.0 / 256.0))
        low = steps - 256.0 * high
        dims = (((1,), (1,)), ((), ()))
        return 256.0 * lax.dot_general(
            pick, high.astype(BF16), dims, preferred_element_type=F32
        ) + lax.dot_general(pick, low.astype(BF16), dims, preferred_element_type=F32)

    for i in range(2):
        pair = [steps_of(2 * i + gg).reshape(-1, 8, 512) for gg in range(2)]
        both = jnp.concatenate(pair, axis=1).astype(jnp.int32).astype(jnp.int16)
        own_send[:, i] = both[:chans]
        src_send[i] = both[chans:]

    pl.semaphore_wait(barrier, chans - 1 + 2 * (segs - 1))

    src_copies, own_copies = [], []
    for d in range(1, chans):
        to = (me + d) % chans
        copy = remote(
            src_send.at[to % 2, to // 2],
            src_recv.at[me, 0],
            src_ss.at[d],
            src_rs.at[d],
            (to, seg),
        )
        copy.start()
        src_copies.append(copy)
    for d in range(1, chans):
        to = (me + d) % chans
        copy = remote(
            own_send.at[to], own_recv.at[me], own_ss.at[d], own_rs.at[d], (to, seg)
        )
        copy.start()
        own_copies.append(copy)
    src_recv[pl.ds(me, 1), 0] = src_send[core, pl.ds(chip, 1)]
    own_recv[pl.ds(me, 1)] = own_send[pl.ds(me, 1)]

    table_hi[:512, :256] = second_hi[0]
    table_hi[512:, :256] = second_hi[1]
    table_hi[:512, 256:] = -second_hi[1]
    table_hi[512:, 256:] = second_hi[0]
    table_lo[:512, :256] = second_lo[0]
    table_lo[512:, :256] = second_lo[1]
    table_lo[:512, 256:] = -second_lo[1]
    table_lo[512:, 256:] = second_lo[0]

    def fill(k1, carry):
        c1 = lag_one[0, pl.ds(k1, 1), :]
        s1 = lag_one[1, pl.ds(k1, 1), :]

        def rows(i, inner):
            r = pl.multiple_of(i * 16, 16)
            c2 = lag_two[0, pl.ds(r, 16), :]
            s2 = lag_two[1, pl.ds(r, 16), :]
            lag_table[k1, pl.ds(r, 16), :] = (c1 * c2 - s1 * s2).astype(BF16)
            lag_table[k1, pl.ds(r + 256, 16), :] = (-(s1 * c2 + c1 * s2)).astype(BF16)
            return inner

        return lax.fori_loop(0, 16, rows, carry)

    lax.fori_loop(0, chans, fill, 0)
    first = iota((16, LAGS), 0) == 0
    head = lag_table[0, :16, :].astype(F32)
    lag_table[0, :16, :] = jnp.where(first, 0.5 * head, head).astype(BF16)

    valid = validity[...].astype(F32).astype(BF16)
    all_segs = valid.shape[0]

    def gate_of(row_seg, row_chan, rows):
        seg_hot = (iota((rows, all_segs), 1) == row_seg).astype(F32).astype(BF16)
        chan_hot = (iota((rows, all_chans), 1) == row_chan).astype(F32)
        return jnp.sum(dot(seg_hot, valid) * chan_hot, axis=1, keepdims=True)

    def named(r, base):
        found = jnp.zeros(r.shape, jnp.int32)
        for s in range(8):
            found = jnp.where(r == s, sources[8 * base + s], found)
        return found

    r32 = iota((32, 1), 0)
    own_gate = gate_of(4 * seg + r32 // 8, 8 * me + r32 % 8, 32)
    r16 = iota((16, 1), 0)
    src_gate = gate_of(4 * seg + 2 * core + r16 // 8, named(r16 % 8, chip), 16)
    want = iota((8, all_chans), 1) == named(iota((8, 1), 0), seg)
    want_valid = lax.dot_general(
        want.astype(F32).astype(BF16),
        valid,
        (((1,), (1,)), ((), ())),
        preferred_element_type=F32,
    ).astype(BF16)
    pairs_all = dot(want_valid, valid)
    shift_hot = (iota((all_chans, 128), 0) == 8 * me + iota((all_chans, 128), 1)).astype(F32)
    pairs = dot(pairs_all.astype(BF16), shift_hot.astype(BF16))
    bins_total = chans * block_len // 2
    scale = 1.0 / jnp.sqrt(2.0 * bins_total * jnp.maximum(pairs, 1.0))

    spread = (iota((256, 256), 0) // 8 == iota((256, 256), 1) // 8).astype(F32).astype(BF16)

    def transform(recv, groups, gate, store):
        rows = 16 * groups

        def sixteen(i, carry):
            units = []
            for p in range(chans):
                last = recv[p, i, :, 384:512].astype(jnp.int32).astype(F32)
                at = block_len - 384
                units.append(jnp.exp2(last[:, at : at + 1] * (1.0 / 128.0)) * (1.0 / STEPS))
            for a in range(0, 512, 128):
                xs = [
                    recv[p, i, :, a : a + 128].astype(jnp.int32).astype(F32) * units[p]
                    for p in range(chans)
                ]
                half = real_dft(xs)
                for k in range(chans):
                    g = half[k] if k <= chans // 2 else conj(half[chans - k])
                    re, im = g
                    c = twist[0, k : k + 1, a : a + 128]
                    s = twist[1, k : k + 1, a : a + 128]
                    if im is None:
                        re, im = re * c, -(re * s)
                    else:
                        re, im = re * c + im * s, im * c - re * s
                    at = pl.ds(pl.multiple_of(k * rows + 16 * i, 16), 16)
                    hi, lo = split(re)
                    h_hi[at, a : a + 128] = hi
                    h_lo[at, a : a + 128] = lo
                    hi, lo = split(im)
                    h_hi[at, 512 + a : 640 + a] = hi
                    h_lo[at, 512 + a : 640 + a] = lo
            return carry

        lax.fori_loop(0, groups, sixteen, 0)

        def second(m, carry):
            at = pl.ds(pl.multiple_of(m * 256, 256), 256)
            hi = h_hi[at, :]
            spec[at, :] = (
                dot(hi, table_hi[...]) + dot(h_lo[at, :], table_hi[...]) + dot(hi, table_lo[...])
            )
            return carry

        lax.fori_loop(0, chans * rows // 256, second, 0)

        def level(k, total):
            at = pl.ds(pl.multiple_of(k * rows, rows), rows)
            re, im = spec[at, :256], spec[at, 256:]
            return total + jnp.sqrt(re * re + im * im)

        total = lax.fori_loop(0, chans, level, jnp.zeros((rows, 256), F32))
        hi, lo = split(total)
        mean = (dot(hi, spread) + dot(lo, spread)) * (1.0 / 128.0) + EPSILON
        factor = gate / mean

        def whiten(k, carry):
            at = pl.ds(pl.multiple_of(k * rows, rows), rows)
            store(k, spec[at, :256] * factor, spec[at, 256:] * factor)
            return carry

        lax.fori_loop(0, chans, whiten, 0)

    def store_src(k, re, im):
        mine[k, :, :256] = re.astype(BF16)
        mine[k, :, 256:] = im.astype(BF16)

    def store_own(k, re, im):
        white[core, k, :, :256] = re.astype(BF16).astype(F32)
        white[core, k, :, 256:] = im.astype(BF16).astype(F32)

    for copy in src_copies:
        copy.wait_recv()
    transform(src_recv, 1, src_gate, store_src)

    per = chans // CHUNKS
    home = core == plane
    slot = 2 * z + core

    def span(ch):
        return pl.ds(ch * per, per)

    def direct(ch, t):
        if t == 0:
            to = partner
        elif t < zs:
            to = device(z + t, plane, plane)
        else:
            to = device(z, 1 - plane, plane)
        return remote(
            mine.at[span(ch)],
            gathered.at[slot, span(ch)],
            ag_ss.at[ch, t],
            ag_rs.at[ch, slot],
            to,
        )

    def slot_of(d, e):
        return 2 * ((z + d) % zs) + (core + e) % 2

    def onward(ch, t):
        d, e = 1 + t // 2, t % 2
        if ch in X_FIRST:
            at, to = slot_of(0, e), device(z + d, plane, core)
        else:
            at, to = slot_of(d, e), device(z, 1 - plane, core)
        ref = gathered.at[at, span(ch)]
        return remote(ref, ref, fw_ss.at[ch, t], ag_rs.at[ch, at], to)

    def arrive(ch, d, e):
        at = slot_of(d, e)
        ref = gathered.at[at, span(ch)]
        remote(ref, ref, fw_ss.at[ch, 0], ag_rs.at[ch, at], partner).wait_recv()

    for ch in range(CHUNKS):
        for t in range(zs, 0, -1):
            direct(ch, t).start()

        @pl.when(jnp.logical_not(home))
        def _(ch=ch):
            direct(ch, 0).start()

    @pl.when(home)
    def _():
        gathered[pl.ds(slot, 1)] = mine[...][None]

    for copy in own_copies:
        copy.wait_recv()
    transform(own_recv, 2, own_gate, store_own)
    white_copy = remote(white.at[core], white.at[core], wh_sem.at[0], wh_sem.at[1], partner)
    white_copy.start()

    acc[...] = jnp.zeros_like(acc)
    prod_b[...] = jnp.zeros_like(prod_b)

    def stack(k, half, prod):
        for oo in range(2):
            o = 2 * half + oo
            for l in range(2):
                re_at, im_at = l * 128, 256 + l * 128
                ar, ai = [], []
                for h in range(2):
                    re = gathered[2 * o + h, k, :, re_at : re_at + 128].astype(F32)
                    im = gathered[2 * o + h, k, :, im_at : im_at + 128].astype(F32)
                    ar += [re[:8], re[8:]]
                    ai += [im[:8], im[8:]]
                for c in range(0, 16, 2):
                    res, ims = [], []
                    for cc in (c, c + 1):
                        re = im = None
                        for g in range(4):
                            at = 8 * g + cc % 8
                            br = white[cc // 8, k, at : at + 1, re_at : re_at + 128]
                            bi = white[cc // 8, k, at : at + 1, im_at : im_at + 128]
                            re = plus(re, ar[g] * br + ai[g] * bi)
                            im = plus(im, ar[g] * bi - ai[g] * br)
                        res.append(re)
                        ims.append(im)
                    at = 128 * oo + 8 * c
                    prod[at : at + 16, re_at : re_at + 128] = jnp.concatenate(res, 0).astype(BF16)
                    prod[at : at + 16, im_at : im_at + 128] = jnp.concatenate(ims, 0).astype(BF16)

    def step(k, carry):
        acc[256:] += dot(prod_b[...], lag_table[jnp.maximum(k - 1, 0)])
        stack(k, 0, prod_a)
        acc[:256] += dot(prod_a[...], lag_table[k])
        stack(k, 1, prod_b)
        return carry

    forwards = 2 * (zs - 1)

    def take(ch, early):
        x_first = ch in X_FIRST

        @pl.when(home)
        def _():
            for d in range(1, zs):
                for e in range(2):
                    if early == (not x_first):
                        arrive(ch, d, e)
                        if early:
                            onward(ch, 2 * (d - 1) + e).start()
            if not early:
                arrive(ch, 0, 1)

        @pl.when(jnp.logical_not(home))
        def _():
            if early == x_first:
                for e in range(2):
                    arrive(ch, 0, e)
            if early and x_first:
                for t in range(forwards):
                    onward(ch, t).start()
            if not early:
                for d in range(1, zs):
                    for e in range(2):
                        arrive(ch, d, e)

    take(0, True)
    white_copy.wait_recv()
    for ch in range(CHUNKS):
        if ch + 1 < CHUNKS:
            take(ch + 1, True)
        take(ch, False)
        lax.fori_loop(ch * per, (ch + 1) * per, step, 0)
    acc[256:] += dot(prod_b[...], lag_table[chans - 1])

    part_send[...] = acc[...].astype(BF16)

    def partial(o, c):
        rows = part_send.at[128 * o + 64 * c : 128 * o + 64 * c + 64]
        to = (2 * chip + c, 2 * o + core)
        return remote(rows, part_recv.at[seg], rs_ss.at[o, c], rs_rs.at[seg], to)

    def remains(o, c):
        return jnp.logical_and(core == c, seg == 2 * o + core)

    for o in range(zs):
        for c in range(2):

            @pl.when(jnp.logical_not(remains(o, c)))
            def _(o=o, c=c):
                partial(o, c).start()

            @pl.when(remains(o, c))
            def _(o=o, c=c):
                part_recv[pl.ds(seg, 1)] = part_send[
                    128 * o + 64 * c : 128 * o + 64 * c + 64
                ][None]

    def landed(d):
        at = (seg + d) % segs
        ref = part_recv.at[at]
        remote(ref, ref, rs_ss.at[0, 0], rs_rs.at[at], partner).wait_recv()

    @pl.when(seg % 2 != core)
    def _():
        landed(0)

    for d in range(1, segs):
        landed(d)
    for c in range(8):
        total = part_recv[0, 8 * c : 8 * c + 8, :].astype(F32)
        for j in range(1, segs):
            total += part_recv[j, 8 * c : 8 * c + 8, :].astype(F32)
        out[:, c, :] = total * scale[:, c : c + 1]

    for copy in src_copies + own_copies:
        copy.wait_send()
    white_copy.wait_send()
    for ch in range(CHUNKS):
        for t in range(1, zs + 1):
            direct(ch, t).wait_send()

        @pl.when(jnp.logical_not(home))
        def _(ch=ch):
            direct(ch, 0).wait_send()

        @pl.when(home != (ch in X_FIRST))
        def _(ch=ch):
            for t in range(forwards):
                onward(ch, t).wait_send()

    for o in range(zs):
        for c in range(2):

            @pl.when(jnp.logical_not(remains(o, c)))
            def _(o=o, c=c):
                partial(o, c).wait_send()


def local(tables, traces, sources, validity):
    chans = lax.axis_size("chan")
    segs = lax.axis_size("seg")
    vmem = pl.BlockSpec(memory_space=pltpu.VMEM)
    dma = pltpu.SemaphoreType.DMA
    return pl.pallas_call(
        body,
        name="correlate",
        out_shape=jax.ShapeDtypeStruct((8, 8, LAGS), F32),
        in_specs=[pl.BlockSpec(memory_space=pltpu.SMEM)] + [vmem] * 7,
        out_specs=vmem,
        scratch_shapes=[
            pltpu.VMEM((chans, 2, 16, 512), jnp.int16),
            pltpu.VMEM((2, chans // 2, 16, 512), jnp.int16),
            pltpu.VMEM((chans, 2, 16, 512), jnp.int16),
            pltpu.VMEM((chans, 1, 16, 512), jnp.int16),
            pltpu.VMEM((32 * chans, 1024), BF16),
            pltpu.VMEM((32 * chans, 1024), BF16),
            pltpu.VMEM((1024, 512), BF16),
            pltpu.VMEM((1024, 512), BF16),
            pltpu.VMEM((32 * chans, 512), F32),
            pltpu.VMEM((2, chans, 32, 512), F32),
            pltpu.VMEM((chans, 16, 512), BF16),
            pltpu.VMEM((8, chans, 16, 512), BF16),
            pltpu.VMEM((chans, 512, LAGS), BF16),
            pltpu.VMEM((256, 512), BF16),
            pltpu.VMEM((256, 512), BF16),
            pltpu.VMEM((512, LAGS), F32),
            pltpu.VMEM((512, LAGS), BF16),
            pltpu.VMEM((segs, 64, LAGS), BF16),
            dma((chans,)),
            dma((chans,)),
            dma((chans,)),
            dma((chans,)),
            dma((CHUNKS, 5)),
            dma((CHUNKS, 6)),
            dma((CHUNKS, 8)),
            dma((2,)),
            dma((4, 2)),
            dma((segs,)),
        ],
        compiler_params=pltpu.CompilerParams(
            collective_id=0, has_side_effects=True, vmem_limit_bytes=60 * 1024 * 1024
        ),
    )(sources, traces.transpose(0, 2, 1), validity, *[jnp.asarray(t) for t in tables])


def solution(mesh):
    chans = mesh.shape["chan"]
    length = 7680
    tables = constant_tables(length, chans)
    return jax.shard_map(
        functools.partial(local, tables),
        mesh=mesh,
        in_specs=(P("seg", None, "chan"), P(), P()),
        out_specs=P("seg", "chan", None),
        check_vma=False,
    )
```

time: 86.1 us -> 64.8 us (0.75)
  the two profiles are of different devices: /device:TPU:1 before, /device:TPU:5 now
where the time goes in v2:
time: 64.8 us; the launch traced here: 64.7 us
  Pallas kernels  63.1 us (97%)
  local copies, waits for them, and re-layouts  1.57 us (2%)
    pallas_call x1, Pallas kernels, local(): pl.pallas_call(body, name='correlate', out_shape=jax.ShapeDtypeStruct((8,...  63.1 us
    unnamed x1, local copies, waits for them, and re-layouts  1.57 us

profile of v2, /device:TPU:5, one launch (start us, length us, event | category | flops | bytes accessed | tf_op | source)
XLA Modules:
  0.0 64.7 jit_solution(16760942427519499866)
XLA Ops:
  0.0 63.1 %correlate.1 = f32[8,8,512]{2,1,0:T(8,128)} custom-call(s32[64]{0:T(128)} %sources.1, f32[4,480,128]{2,1,0:T(8,128)} %bitcast.1, s32[32,128]{1,0:T(8,128)} %validity.1, f32[2,16,512]{2,1,0:T(8,128)} %constant.10.clone.twist, bf16[2,512,256]{2,1,0:T(8,128)(2,1)} %constant.11.clone.second_hi, bf16[2,512,256]{2,1,0:T(8,128)(2,1)} %constant.12.clone.second_lo, ...), custom_call_target="tpu_custom_call" | custom-call | tf_op jit(solution)/shard_map/correlate/pallas_call | solution.py:569
  63.1 1.6 %copy.10 = f32[8,8,512]{2,1,0:T(8,128)} copy(f32[8,8,512]{2,1,0:T(8,128)} %correlate.1) | data formatting | bytes 262144

commit v3 on v2

v3 whole, which is shorter than its diff:
```python
import functools
import math

import jax
import jax.numpy as jnp
import numpy as np
from jax import lax
from jax.experimental import pallas as pl
from jax.experimental.pallas import tpu as pltpu
from jax.sharding import PartitionSpec as P

LAGS = 512
EPSILON = 1e-06
MESH = pl.DeviceIdType.MESH
CHUNKS = 8
STEPS = 32000.0
F32 = jnp.float32
BF16 = jnp.bfloat16


def constant_tables(length, blocks):
    block_len = length // blocks
    half = block_len // 2
    q = np.arange(block_len)[:, None]
    k1 = np.arange(blocks)[:, None]
    k2 = np.arange(half)[None, :]
    angle = 2.0 * math.pi / length * ((k1 * q.T) % length)
    twist = np.zeros((2, blocks, 512), np.float32)
    twist[0, :, :block_len] = np.cos(angle)
    twist[1, :, :block_len] = np.sin(angle)
    angle = 2.0 * math.pi / block_len * ((q * k2) % block_len)
    second = np.zeros((2, 512, 256), np.float32)
    second[0, :block_len, :half] = np.cos(angle)
    second[1, :block_len, :half] = np.sin(angle)
    second_hi = second.astype(jnp.bfloat16)
    second_lo = (second - second_hi.astype(np.float32)).astype(jnp.bfloat16)
    lag = (np.arange(LAGS) - LAGS // 2)[None, :]
    angle = 2.0 * math.pi / length * ((k1 * lag) % length)
    lag_one = np.stack([np.cos(angle), np.sin(angle)]).astype(np.float32)
    angle = 2.0 * math.pi / block_len * ((k2.T * lag) % block_len)
    lag_two = np.zeros((2, 256, LAGS), np.float32)
    lag_two[0, :half] = 2.0 * np.cos(angle)
    lag_two[1, :half] = 2.0 * np.sin(angle)
    return twist, second_hi, second_lo, lag_one, lag_two


def times_root(value, k, n):
    re, im = value
    c, s = math.cos(2.0 * math.pi * k / n), math.sin(2.0 * math.pi * k / n)
    if k == 0:
        return value
    if 4 * k == n:
        return (im, -re)
    if 2 * k == n:
        return (-re, None if im is None else -im)
    if im is None:
        return (re * c, re * (-s))
    return (re * c + im * s, im * c - re * s)


def plus(a, b):
    if a is None:
        return b
    return a if b is None else a + b


def conj(value):
    re, im = value
    return (re, None if im is None else -im)


def real_dft(xs):
    n = len(xs)
    if n == 2:
        return [(xs[0] + xs[1], None), (xs[0] - xs[1], None)]
    even, odd = real_dft(xs[0::2]), real_dft(xs[1::2])
    h = n // 2
    out = []
    for k in range(h + 1):
        i = k % h
        e = even[i] if i <= h // 2 else conj(even[h - i])
        o = odd[i] if i <= h // 2 else conj(odd[h - i])
        t = times_root(o, k, n)
        out.append((plus(e[0], t[0]), plus(e[1], t[1])))
    return out


def split(value):
    hi = value.astype(BF16)
    return hi, (value - hi.astype(F32)).astype(BF16)


def dot(a, b):
    return jnp.dot(a, b, preferred_element_type=F32)


def body(
    sources,
    traces,
    validity,
    twist_in,
    second_hi,
    second_lo,
    lag_one,
    lag_two,
    out,
    names_smem,
    staged,
    valid_in,
    twist,
    sec_hi,
    sec_lo,
    one,
    two,
    own_send,
    src_send,
    own_recv,
    src_recv,
    h_hi,
    h_lo,
    table_hi,
    table_lo,
    spec,
    white,
    white_send,
    white_recv,
    gathered,
    lag_table,
    prod_a,
    prod_b,
    acc,
    part_send,
    part_recv,
    in_sem,
    own_ss,
    own_rs,
    src_ss,
    src_rs,
    ag_ss,
    fw_ss,
    ag_rs,
    wh_ss,
    wh_rs,
    rs_ss,
    rs_rs,
):
    chans = lax.axis_size("chan")
    segs = lax.axis_size("seg")
    me = lax.axis_index("chan")
    seg = lax.axis_index("seg")
    chip = me // 2
    core = me % 2
    z = chip // 2
    plane = chip % 2
    zs = chans // 4
    block_len = traces.shape[1]
    partner = (2 * chip + 1 - core, seg)

    def iota(shape, axis):
        return lax.broadcasted_iota(jnp.int32, shape, axis)

    def remote(src, dst, send, recv, to):
        return pltpu.make_async_remote_copy(
            src_ref=src,
            dst_ref=dst,
            send_sem=send,
            recv_sem=recv,
            device_id=to,
            device_id_type=MESH,
        )

    def device(zz, pp, cc):
        return (zz % zs) * 4 + pp * 2 + cc

    def octet_of(zz, pp):
        return 2 * zz + (zz + pp) % 2

    fetch = [
        pltpu.make_async_copy(a, b, in_sem.at[n])
        for n, (a, b) in enumerate(
            [(traces.at[g], staged.at[g]) for g in range(4)]
            + [
                (sources, names_smem),
                (validity, valid_in),
                (twist_in, twist),
                (second_hi, sec_hi),
                (second_lo, sec_lo),
                (lag_one, one),
                (lag_two, two),
            ]
        )
    ]
    for n in (4, 0, 1, 2, 3, 7, 8, 9, 10, 5, 6):
        fetch[n].start()

    barrier = pltpu.get_barrier_semaphore()
    for d in range(1, chans):
        pl.semaphore_signal(
            barrier, inc=1, device_id=((me + d) % chans, seg), device_id_type=MESH
        )
    for d in range(1, segs):
        for p in range(2):
            pl.semaphore_signal(
                barrier,
                inc=1,
                device_id=(device(z, p, core), (seg + d) % segs),
                device_id_type=MESH,
            )

    fetch[4].wait()
    all_chans = staged.shape[2]
    count = 8 * chans // 2
    names = jnp.zeros((count, 1), jnp.int32)
    r_names = iota((count, 1), 0)
    for s in range(count):
        names = jnp.where(r_names == s, names_smem[s], names)
    row = iota((all_chans, 1), 0)
    pick = jnp.concatenate([row, names], 0)
    pick = (iota((all_chans + count, all_chans), 1) == pick).astype(F32).astype(BF16)

    def steps_of(g):
        fetch[g].wait()
        x = staged[g]
        top = jnp.maximum(jnp.max(jnp.abs(x), axis=0, keepdims=True), 1e-30)
        power = jnp.ceil(jnp.log(top) * (128.0 / math.log(2.0))) + 1.0
        steps = jnp.round(x * (STEPS / jnp.exp2(power * (1.0 / 128.0))))
        tail = jnp.where(iota((512 - block_len, all_chans), 0) == 0, power, 0.0)
        steps = jnp.concatenate([steps, tail], 0)
        high = jnp.round(steps * (1.0 / 256.0))
        low = steps - 256.0 * high
        dims = (((1,), (1,)), ((), ()))
        return 256.0 * lax.dot_general(
            pick, high.astype(BF16), dims, preferred_element_type=F32
        ) + lax.dot_general(pick, low.astype(BF16), dims, preferred_element_type=F32)

    for i in range(2):
        pair = [steps_of(2 * i + gg).reshape(-1, 8, 512) for gg in range(2)]
        both = jnp.concatenate(pair, axis=1).astype(jnp.int32).astype(jnp.int16)
        own_send[i] = both[:chans]
        src_send[i] = both[chans:]

    pl.semaphore_wait(barrier, chans - 1 + 2 * (segs - 1))

    src_copies, own_copies = [], [[], []]
    for d in range(1, chans):
        to = (me + d) % chans
        copy = remote(
            src_send.at[to % 2, octet_of(to // 4, (to // 2) % 2)],
            src_recv.at[me],
            src_ss.at[d],
            src_rs.at[d],
            (to, seg),
        )
        copy.start()
        src_copies.append(copy)
    for i in range(2):
        for d in range(1, chans):
            to = (me + d) % chans
            copy = remote(
                own_send.at[i, to],
                own_recv.at[i, me],
                own_ss.at[i, d],
                own_rs.at[i, d],
                (to, seg),
            )
            copy.start()
            own_copies[i].append(copy)
    src_recv[pl.ds(me, 1)] = src_send[core, pl.ds(octet_of(z, plane), 1)]
    for i in range(2):
        own_recv[i, pl.ds(me, 1)] = own_send[i, pl.ds(me, 1)]

    for n in range(5, 11):
        fetch[n].wait()

    table_hi[:512, :256] = sec_hi[0]
    table_hi[512:, :256] = sec_hi[1]
    table_hi[:512, 256:] = -sec_hi[1]
    table_hi[512:, 256:] = sec_hi[0]
    table_lo[:512, :256] = sec_lo[0]
    table_lo[512:, :256] = sec_lo[1]
    table_lo[:512, 256:] = -sec_lo[1]
    table_lo[512:, 256:] = sec_lo[0]

    def fill(k1, carry):
        c1 = one[0, pl.ds(k1, 1), :]
        s1 = one[1, pl.ds(k1, 1), :]

        def rows(i, inner):
            r = pl.multiple_of(i * 16, 16)
            c2 = two[0, pl.ds(r, 16), :]
            s2 = two[1, pl.ds(r, 16), :]
            lag_table[k1, pl.ds(r, 16), :] = (c1 * c2 - s1 * s2).astype(BF16)
            lag_table[k1, pl.ds(r + 256, 16), :] = (-(s1 * c2 + c1 * s2)).astype(BF16)
            return inner

        return lax.fori_loop(0, 16, rows, carry)

    lax.fori_loop(0, chans, fill, 0)
    first = iota((16, LAGS), 0) == 0
    head = lag_table[0, :16, :].astype(F32)
    lag_table[0, :16, :] = jnp.where(first, 0.5 * head, head).astype(BF16)

    valid = valid_in[...].astype(F32).astype(BF16)
    all_segs = valid.shape[0]

    def gate_of(row_seg, row_chan, rows):
        seg_hot = (iota((rows, all_segs), 1) == row_seg).astype(F32).astype(BF16)
        chan_hot = (iota((rows, all_chans), 1) == row_chan).astype(F32)
        return jnp.sum(dot(seg_hot, valid) * chan_hot, axis=1, keepdims=True)

    def named(r, base):
        found = jnp.zeros(r.shape, jnp.int32)
        for s in range(8):
            found = jnp.where(r == s, names_smem[8 * base + s], found)
        return found

    r16 = iota((16, 1), 0)
    own_gates = [
        gate_of(4 * seg + 2 * i + r16 // 8, 8 * me + r16 % 8, 16) for i in range(2)
    ]
    src_gate = gate_of(4 * seg + 2 * core + r16 // 8, named(r16 % 8, octet_of(z, plane)), 16)
    want = iota((8, all_chans), 1) == named(iota((8, 1), 0), seg)
    want_valid = lax.dot_general(
        want.astype(F32).astype(BF16),
        valid,
        (((1,), (1,)), ((), ())),
        preferred_element_type=F32,
    ).astype(BF16)
    pairs_all = dot(want_valid, valid)
    shift_hot = (iota((all_chans, 128), 0) == 8 * me + iota((all_chans, 128), 1)).astype(F32)
    pairs = dot(pairs_all.astype(BF16), shift_hot.astype(BF16))
    bins_total = chans * block_len // 2
    scale = 1.0 / jnp.sqrt(2.0 * bins_total * jnp.maximum(pairs, 1.0))

    spread = (iota((256, 256), 0) // 8 == iota((256, 256), 1) // 8).astype(F32).astype(BF16)

    def transform(recv, gate, store):
        units = []
        for p in range(chans):
            last = recv[p, :, 384:512].astype(jnp.int32).astype(F32)
            at = block_len - 384
            units.append(jnp.exp2(last[:, at : at + 1] * (1.0 / 128.0)) * (1.0 / STEPS))
        for a in range(0, 512, 128):
            xs = [
                recv[p, :, a : a + 128].astype(jnp.int32).astype(F32) * units[p]
                for p in range(chans)
            ]
            half = real_dft(xs)
            for k in range(chans):
                g = half[k] if k <= chans // 2 else conj(half[chans - k])
                re, im = g
                c = twist[0, k : k + 1, a : a + 128]
                s = twist[1, k : k + 1, a : a + 128]
                if im is None:
                    re, im = re * c, -(re * s)
                else:
                    re, im = re * c + im * s, im * c - re * s
                at = slice(16 * k, 16 * k + 16)
                hi, lo = split(re)
                h_hi[at, a : a + 128] = hi
                h_lo[at, a : a + 128] = lo
                hi, lo = split(im)
                h_hi[at, 512 + a : 640 + a] = hi
                h_lo[at, 512 + a : 640 + a] = lo
        spec[...] = (
            dot(h_hi[...], table_hi[...])
            + dot(h_lo[...], table_hi[...])
            + dot(h_hi[...], table_lo[...])
        )
        total = None
        for k in range(chans):
            re, im = spec[16 * k : 16 * k + 16, :256], spec[16 * k : 16 * k + 16, 256:]
            total = plus(total, jnp.sqrt(re * re + im * im))
        hi, lo = split(total)
        mean = (dot(hi, spread) + dot(lo, spread)) * (1.0 / 128.0) + EPSILON
        factor = gate / mean
        for k in range(chans):
            for part in range(2):
                at = slice(256 * part, 256 * part + 256)
                store(k, at, (spec[16 * k : 16 * k + 16, at] * factor).astype(BF16))

    per = chans // CHUNKS
    slot = 2 * z + core

    def span(ch):
        return pl.ds(ch * per, per)

    def store_src(k, at, value):
        gathered[slot, k, :, at] = value

    for copy in src_copies:
        copy.wait_recv()
    transform(src_recv, src_gate, store_src)

    def gather(ch, d):
        ref = gathered.at[slot, span(ch)]
        to = partner if d == 0 else (device(z + d, plane, core), seg)
        return remote(ref, ref, ag_ss.at[ch, d], ag_rs.at[ch, slot], to)

    def slot_of(d, cc):
        return 2 * ((z + d) % zs) + cc

    def forward(ch, d):
        at = slot_of(d, core)
        ref = gathered.at[at, span(ch)]
        return remote(ref, ref, fw_ss.at[ch, d], ag_rs.at[ch, at], partner)

    def arrive(ch, d, cc):
        at = slot_of(d, cc)
        ref = gathered.at[at, span(ch)]
        remote(ref, ref, fw_ss.at[ch, 0], ag_rs.at[ch, at], partner).wait_recv()

    for ch in range(CHUNKS):
        for d in range(zs - 1, -1, -1):
            gather(ch, d).start()

    across = (device(z, 1 - plane, core), seg)

    def cross(i, ch):
        return remote(
            white_send.at[i, span(ch)],
            white_recv.at[i, span(ch)],
            wh_ss.at[i, ch],
            wh_rs.at[i, ch],
            across,
        )

    for i in range(2):

        def store_own(k, at, value, i=i):
            white_send[i, k, :, at] = value
            white[plane, k, 16 * i : 16 * i + 16, at] = value.astype(F32)

        for copy in own_copies[i]:
            copy.wait_recv()
        transform(own_recv.at[i], own_gates[i], store_own)
        for ch in range(CHUNKS):
            cross(i, ch).start()

    acc[...] = jnp.zeros_like(acc)
    prod_b[...] = jnp.zeros_like(prod_b)

    def stack(k, half, prod):
        for oo in range(2):
            o = 2 * half + oo
            for l in range(2):
                re_at, im_at = l * 128, 256 + l * 128
                ar, ai = [], []
                for h in range(2):
                    re = gathered[2 * o + h, k, :, re_at : re_at + 128].astype(F32)
                    im = gathered[2 * o + h, k, :, im_at : im_at + 128].astype(F32)
                    ar += [re[:8], re[8:]]
                    ai += [im[:8], im[8:]]
                for c in range(0, 16, 2):
                    res, ims = [], []
                    for cc in (c, c + 1):
                        re = im = None
                        for g in range(4):
                            at = 8 * g + cc % 8
                            br = white[cc // 8, k, at : at + 1, re_at : re_at + 128]
                            bi = white[cc // 8, k, at : at + 1, im_at : im_at + 128]
                            re = plus(re, ar[g] * br + ai[g] * bi)
                            im = plus(im, ar[g] * bi - ai[g] * br)
                        res.append(re)
                        ims.append(im)
                    at = 128 * oo + 8 * c
                    prod[at : at + 16, re_at : re_at + 128] = jnp.concatenate(res, 0).astype(BF16)
                    prod[at : at + 16, im_at : im_at + 128] = jnp.concatenate(ims, 0).astype(BF16)

    def step(k, carry):
        acc[256:] += dot(prod_b[...], lag_table[jnp.maximum(k - 1, 0)])
        stack(k, 0, prod_a)
        acc[:256] += dot(prod_a[...], lag_table[k])
        stack(k, 1, prod_b)
        return carry


    def relay(ch):
        for d in range(1, zs):
            arrive(ch, d, core)
            forward(ch, d).start()

    def widen(k, carry):
        for i in range(2):
            white[1 - plane, k, 16 * i : 16 * i + 16, :] = white_recv[i, k].astype(F32)
        return carry

    relay(0)
    for ch in range(CHUNKS):
        if ch + 1 < CHUNKS:
            relay(ch + 1)
        for d in range(zs):
            arrive(ch, d, 1 - core)
        for i in range(2):
            cross(i, ch).wait_recv()
        lax.fori_loop(ch * per, (ch + 1) * per, widen, 0)
        lax.fori_loop(ch * per, (ch + 1) * per, step, 0)
    acc[256:] += dot(prod_b[...], lag_table[chans - 1])

    part_send[...] = acc[...].astype(BF16)

    def partial(o, p):
        rows = part_send.at[128 * o + 64 * p : 128 * o + 64 * p + 64]
        to = (device(z, p, core), octet_of(o, plane))
        return remote(rows, part_recv.at[seg], rs_ss.at[o, p], rs_rs.at[seg], to)

    def remains(o, p):
        return jnp.logical_and(plane == p, seg == octet_of(o, plane))

    for o in range(zs):
        for p in range(2):

            @pl.when(jnp.logical_not(remains(o, p)))
            def _(o=o, p=p):
                partial(o, p).start()

            @pl.when(remains(o, p))
            def _(o=o, p=p):
                part_recv[pl.ds(seg, 1)] = part_send[
                    128 * o + 64 * p : 128 * o + 64 * p + 64
                ][None]

    def landed(d):
        at = (seg + d) % segs
        ref = part_recv.at[at]
        remote(ref, ref, rs_ss.at[0, 0], rs_rs.at[at], partner).wait_recv()

    @pl.when((seg + seg // 2) % 2 != plane)
    def _():
        landed(0)

    for d in range(1, segs):
        landed(d)
    for c in range(8):
        total = part_recv[0, 8 * c : 8 * c + 8, :].astype(F32)
        for j in range(1, segs):
            total += part_recv[j, 8 * c : 8 * c + 8, :].astype(F32)
        out[:, c, :] = total * scale[:, c : c + 1]

    for copy in src_copies + own_copies[0] + own_copies[1]:
        copy.wait_send()
    for ch in range(CHUNKS):
        for d in range(zs):
            gather(ch, d).wait_send()
        for d in range(1, zs):
            forward(ch, d).wait_send()
        for i in range(2):
            cross(i, ch).wait_send()
    for o in range(zs):
        for p in range(2):

            @pl.when(jnp.logical_not(remains(o, p)))
            def _(o=o, p=p):
                partial(o, p).wait_send()


def local(tables, traces, sources, validity):
    chans = lax.axis_size("chan")
    segs = lax.axis_size("seg")
    vmem = pl.BlockSpec(memory_space=pltpu.VMEM)
    hbm = pl.BlockSpec(memory_space=pl.ANY)
    dma = pltpu.SemaphoreType.DMA
    turned = traces.transpose(0, 2, 1)
    tables = [jnp.asarray(t) for t in tables]
    return pl.pallas_call(
        body,
        name="correlate",
        out_shape=jax.ShapeDtypeStruct((8, 8, LAGS), F32),
        in_specs=[hbm] * 8,
        out_specs=vmem,
        scratch_shapes=[
            pltpu.SMEM(sources.shape, jnp.int32),
            pltpu.VMEM(turned.shape, F32),
            pltpu.VMEM(validity.shape, jnp.int32),
            *[pltpu.VMEM(t.shape, t.dtype) for t in tables],
            pltpu.VMEM((2, chans, 16, 512), jnp.int16),
            pltpu.VMEM((2, chans // 2, 16, 512), jnp.int16),
            pltpu.VMEM((2, chans, 16, 512), jnp.int16),
            pltpu.VMEM((chans, 16, 512), jnp.int16),
            pltpu.VMEM((16 * chans, 1024), BF16),
            pltpu.VMEM((16 * chans, 1024), BF16),
            pltpu.VMEM((1024, 512), BF16),
            pltpu.VMEM((1024, 512), BF16),
            pltpu.VMEM((16 * chans, 512), F32),
            pltpu.VMEM((2, chans, 32, 512), F32),
            pltpu.VMEM((2, chans, 16, 512), BF16),
            pltpu.VMEM((2, chans, 16, 512), BF16),
            pltpu.VMEM((8, chans, 16, 512), BF16),
            pltpu.VMEM((chans, 512, LAGS), BF16),
            pltpu.VMEM((256, 512), BF16),
            pltpu.VMEM((256, 512), BF16),
            pltpu.VMEM((512, LAGS), F32),
            pltpu.VMEM((512, LAGS), BF16),
            pltpu.VMEM((segs, 64, LAGS), BF16),
            dma((11,)),
            dma((2, chans)),
            dma((2, chans)),
            dma((chans,)),
            dma((chans,)),
            dma((CHUNKS, 4)),
            dma((CHUNKS, 4)),
            dma((CHUNKS, 8)),
            dma((2, CHUNKS)),
            dma((2, CHUNKS)),
            dma((4, 2)),
            dma((segs,)),
        ],
        compiler_params=pltpu.CompilerParams(
            collective_id=0, has_side_effects=True, vmem_limit_bytes=60 * 1024 * 1024
        ),
    )(sources, turned, validity, *tables)


def solution(mesh):
    chans = mesh.shape["chan"]
    length = 7680
    tables = constant_tables(length, chans)
    return jax.shard_map(
        functools.partial(local, tables),
        mesh=mesh,
        in_specs=(P("seg", None, "chan"), P(), P()),
        out_specs=P("seg", "chan", None),
        check_vma=False,
    )
```

time: 64.8 us -> 56.3 us (0.87)
  the two profiles are of different devices: /device:TPU:5 before, /device:TPU:1 now
where the time goes in v3:
time: 56.3 us; the launch traced here: 55.7 us
  Pallas kernels  54.2 us (96%)
  local copies, waits for them, and re-layouts  1.57 us (3%)
    pallas_call x1, Pallas kernels, local(): pl.pallas_call(body, name='correlate', out_shape=jax.ShapeDtypeStruct((8,...  54.2 us
    unnamed x1, local copies, waits for them, and re-layouts  1.57 us

profile of v3, /device:TPU:1, one launch (start us, length us, event | category | flops | bytes accessed | tf_op | source)
XLA Modules:
  0.0 55.7 jit_solution(16796345201973451480)
XLA Ops:
  0.0 54.2 %correlate.1 = f32[8,8,512]{2,1,0:T(8,128)} custom-call(s32[64]{0:T(128)} %sources.1, f32[4,480,128]{2,1,0:T(8,128)} %bitcast.1, s32[32,128]{1,0:T(8,128)} %validity.1, f32[2,16,512]{2,1,0:T(8,128)} %constant.10.clone.twist_in, bf16[2,512,256]{2,1,0:T(8,128)(2,1)} %constant.11.clone.second_hi, bf16[2,512,256]{2,1,0:T(8,128)(2,1)} %constant.12.clone.second_lo, ...), custom_call_target="tpu_custom_call" | custom-call | tf_op jit(solution)/shard_map/correlate/pallas_call | solution.py:565
  54.2 1.6 %copy.10 = f32[8,8,512]{2,1,0:T(8,128)} copy(f32[8,8,512]{2,1,0:T(8,128)} %correlate.1) | data formatting | bytes 262144

commit v4 on v3

--- a/solution.py
+++ b/solution.py
@@ -175,6 +175,20 @@
     def octet_of(zz, pp):
         return 2 * zz + (zz + pp) % 2
 
+    barrier = pltpu.get_barrier_semaphore()
+    for d in sorted(range(1, chans), key=lambda d: abs(d - chans // 2)):
+        pl.semaphore_signal(
+            barrier, inc=1, device_id=((me + d) % chans, seg), device_id_type=MESH
+        )
+    for d in range(1, segs):
+        for p in range(2):
+            pl.semaphore_signal(
+                barrier,
+                inc=1,
+                device_id=(device(z, p, core), (seg + d) % segs),
+                device_id_type=MESH,
+            )
+
     fetch = [
         pltpu.make_async_copy(a, b, in_sem.at[n])
         for n, (a, b) in enumerate(
@@ -192,20 +206,6 @@
     ]
     for n in (4, 0, 1, 2, 3, 7, 8, 9, 10, 5, 6):
         fetch[n].start()
-
-    barrier = pltpu.get_barrier_semaphore()
-    for d in range(1, chans):
-        pl.semaphore_signal(
-            barrier, inc=1, device_id=((me + d) % chans, seg), device_id_type=MESH
-        )
-    for d in range(1, segs):
-        for p in range(2):
-            pl.semaphore_signal(
-                barrier,
-                inc=1,
-                device_id=(device(z, p, core), (seg + d) % segs),
-                device_id_type=MESH,
-            )
 
     fetch[4].wait()
     all_chans = staged.shape[2]
@@ -289,16 +289,20 @@
             r = pl.multiple_of(i * 16, 16)
             c2 = two[0, pl.ds(r, 16), :]
             s2 = two[1, pl.ds(r, 16), :]
-            lag_table[k1, pl.ds(r, 16), :] = (c1 * c2 - s1 * s2).astype(BF16)
-            lag_table[k1, pl.ds(r + 256, 16), :] = (-(s1 * c2 + c1 * s2)).astype(BF16)
+            c = c1 * c2 - s1 * s2
+            s = s1 * c2 + c1 * s2
+            lag_table[k1, pl.ds(r, 16), :] = (c - s).astype(BF16)
+            lag_table[k1, pl.ds(r + 256, 16), :] = s.astype(BF16)
+            lag_table[k1, pl.ds(r + 512, 16), :] = (-c).astype(BF16)
             return inner
 
         return lax.fori_loop(0, 16, rows, carry)
 
     lax.fori_loop(0, chans, fill, 0)
     first = iota((16, LAGS), 0) == 0
-    head = lag_table[0, :16, :].astype(F32)
-    lag_table[0, :16, :] = jnp.where(first, 0.5 * head, head).astype(BF16)
+    for r in (0, 256, 512):
+        head = lag_table[0, r : r + 16, :].astype(F32)
+        lag_table[0, r : r + 16, :] = jnp.where(first, 0.5 * head, head).astype(BF16)
 
     valid = valid_in[...].astype(F32).astype(BF16)
     all_segs = valid.shape[0]
@@ -414,6 +418,9 @@
         for d in range(zs - 1, -1, -1):
             gather(ch, d).start()
 
+    rest = [(1, ch) for ch in range(CHUNKS)]
+    for ch in range(3, CHUNKS):
+        rest.insert(2 * ch - 3, (0, ch))
     across = (device(z, 1 - plane, core), seg)
 
     def cross(i, ch):
@@ -434,70 +441,80 @@
         for copy in own_copies[i]:
             copy.wait_recv()
         transform(own_recv.at[i], own_gates[i], store_own)
-        for ch in range(CHUNKS):
-            cross(i, ch).start()
+        for pair in [(0, ch) for ch in range(3)] if i == 0 else rest:
+            cross(*pair).start()
 
     acc[...] = jnp.zeros_like(acc)
     prod_b[...] = jnp.zeros_like(prod_b)
 
     def stack(k, half, prod):
-        for oo in range(2):
-            o = 2 * half + oo
-            for l in range(2):
-                re_at, im_at = l * 128, 256 + l * 128
-                ar, ai = [], []
+        for l in range(2):
+            re_at, im_at = l * 128, 256 + l * 128
+            ar, ap, am = [], [], []
+            for oo in range(2):
                 for h in range(2):
-                    re = gathered[2 * o + h, k, :, re_at : re_at + 128].astype(F32)
-                    im = gathered[2 * o + h, k, :, im_at : im_at + 128].astype(F32)
-                    ar += [re[:8], re[8:]]
-                    ai += [im[:8], im[8:]]
-                for c in range(0, 16, 2):
-                    res, ims = [], []
-                    for cc in (c, c + 1):
-                        re = im = None
-                        for g in range(4):
-                            at = 8 * g + cc % 8
-                            br = white[cc // 8, k, at : at + 1, re_at : re_at + 128]
-                            bi = white[cc // 8, k, at : at + 1, im_at : im_at + 128]
-                            re = plus(re, ar[g] * br + ai[g] * bi)
-                            im = plus(im, ar[g] * bi - ai[g] * br)
-                        res.append(re)
-                        ims.append(im)
-                    at = 128 * oo + 8 * c
-                    prod[at : at + 16, re_at : re_at + 128] = jnp.concatenate(res, 0).astype(BF16)
-                    prod[at : at + 16, im_at : im_at + 128] = jnp.concatenate(ims, 0).astype(BF16)
-
-    def step(k, carry):
-        acc[256:] += dot(prod_b[...], lag_table[jnp.maximum(k - 1, 0)])
-        stack(k, 0, prod_a)
-        acc[:256] += dot(prod_a[...], lag_table[k])
-        stack(k, 1, prod_b)
-        return carry
-
+                    slot_at = 2 * (2 * half + oo) + h
+                    re = gathered[slot_at, k, :, re_at : re_at + 128].astype(F32)
+                    im = gathered[slot_at, k, :, im_at : im_at + 128].astype(F32)
+                    for part in (slice(0, 8), slice(8, 16)):
+                        ar.append(re[part])
+                        ap.append(re[part] + im[part])
+                        am.append(re[part] - im[part])
+            for c in range(0, 16, 2):
+                rows = [[[], [], []], [[], [], []]]
+                for cc in (c, c + 1):
+                    sums = [[None] * 3, [None] * 3]
+                    for g in range(4):
+                        at = 8 * g + cc % 8
+                        br = white[cc // 8, k, at : at + 1, re_at : re_at + 128]
+                        bi = white[cc // 8, k, at : at + 1, im_at : im_at + 128]
+                        bs = br + bi
+                        for oo in range(2):
+                            n = 4 * oo + g
+                            sums[oo] = [
+                                plus(sums[oo][0], ar[n] * bs),
+                                plus(sums[oo][1], ap[n] * br),
+                                plus(sums[oo][2], am[n] * bi),
+                            ]
+                    for oo in range(2):
+                        for m in range(3):
+                            rows[oo][m].append(sums[oo][m])
+                for oo in range(2):
+                    at = 256 * half + 128 * oo + 8 * c
+                    for m in range(3):
+                        lane = 256 * m + 128 * l
+                        prod[at : at + 16, lane : lane + 128] = jnp.concatenate(
+                            rows[oo][m], 0
+                        ).astype(BF16)
 
     def relay(ch):
         for d in range(1, zs):
             arrive(ch, d, core)
             forward(ch, d).start()
 
-    def widen(k, carry):
-        for i in range(2):
-            white[1 - plane, k, 16 * i : 16 * i + 16, :] = white_recv[i, k].astype(F32)
-        return carry
-
-    relay(0)
-    for ch in range(CHUNKS):
-        if ch + 1 < CHUNKS:
-            relay(ch + 1)
+    def ready(ch):
         for d in range(zs):
             arrive(ch, d, 1 - core)
         for i in range(2):
             cross(i, ch).wait_recv()
-        lax.fori_loop(ch * per, (ch + 1) * per, widen, 0)
-        lax.fori_loop(ch * per, (ch + 1) * per, step, 0)
-    acc[256:] += dot(prod_b[...], lag_table[chans - 1])
-
-    part_send[...] = acc[...].astype(BF16)
+            for j in range(per):
+                k = ch * per + j
+                white[1 - plane, k, 16 * i : 16 * i + 16, :] = white_recv[i, k].astype(F32)
+
+    bufs = [prod_a, prod_b]
+
+    def chunk(ch, carry):
+        relay(ch + 1)
+        ready(ch)
+        for j in range(per):
+            k = ch * per + j
+            acc[...] += dot(bufs[1 - j % 2][...], lag_table[jnp.maximum(k - 1, 0)])
+            stack(k, 0, bufs[j % 2])
+            stack(k, 1, bufs[j % 2])
+        return carry
+
+    relay(0)
+    lax.fori_loop(0, CHUNKS - 1, chunk, 0)
 
     def partial(o, p):
         rows = part_send.at[128 * o + 64 * p : 128 * o + 64 * p + 64]
@@ -507,35 +524,40 @@
     def remains(o, p):
         return jnp.logical_and(plane == p, seg == octet_of(o, plane))
 
-    for o in range(zs):
-        for p in range(2):
-
-            @pl.when(jnp.logical_not(remains(o, p)))
-            def _(o=o, p=p):
-                partial(o, p).start()
-
-            @pl.when(remains(o, p))
-            def _(o=o, p=p):
-                part_recv[pl.ds(seg, 1)] = part_send[
-                    128 * o + 64 * p : 128 * o + 64 * p + 64
-                ][None]
-
-    def landed(d):
-        at = (seg + d) % segs
-        ref = part_recv.at[at]
-        remote(ref, ref, rs_ss.at[0, 0], rs_rs.at[at], partner).wait_recv()
-
-    @pl.when((seg + seg // 2) % 2 != plane)
-    def _():
-        landed(0)
-
-    for d in range(1, segs):
-        landed(d)
-    for c in range(8):
-        total = part_recv[0, 8 * c : 8 * c + 8, :].astype(F32)
-        for j in range(1, segs):
-            total += part_recv[j, 8 * c : 8 * c + 8, :].astype(F32)
-        out[:, c, :] = total * scale[:, c : c + 1]
+    def scatter(half):
+        part_send[256 * half : 256 * half + 256] = acc[256 * half : 256 * half + 256].astype(BF16)
+        for o in (2 * half, 2 * half + 1):
+            for p in range(2):
+
+                @pl.when(jnp.logical_not(remains(o, p)))
+                def _(o=o, p=p):
+                    partial(o, p).start()
+
+                @pl.when(remains(o, p))
+                def _(o=o, p=p):
+                    part_recv[pl.ds(seg, 1)] = part_send[
+                        128 * o + 64 * p : 128 * o + 64 * p + 64
+                    ][None]
+
+    ready(CHUNKS - 1)
+    last = chans - per
+
+    def lags(half, k, prod):
+        at = slice(256 * half, 256 * half + 256)
+        acc[at] += dot(prod[at, :], lag_table[k])
+
+    stack(last, 0, prod_a)
+    for half in range(2):
+        lags(half, last - 1, prod_b)
+    stack(last + 1, 0, prod_b)
+    lags(0, last, prod_a)
+    stack(last, 1, prod_a)
+    lags(0, last + 1, prod_b)
+    scatter(0)
+    stack(last + 1, 1, prod_b)
+    lags(1, last, prod_a)
+    lags(1, last + 1, prod_b)
+    scatter(1)
 
     for copy in src_copies + own_copies[0] + own_copies[1]:
         copy.wait_send()
@@ -546,6 +568,23 @@
             forward(ch, d).wait_send()
         for i in range(2):
             cross(i, ch).wait_send()
+    def landed(d):
+        at = (seg + d) % segs
+        ref = part_recv.at[at]
+        remote(ref, ref, rs_ss.at[0, 0], rs_rs.at[at], partner).wait_recv()
+
+    @pl.when((seg + seg // 2) % 2 != plane)
+    def _():
+        landed(0)
+
+    for d in range(1, segs):
+        landed(d)
+    for c in range(8):
+        total = part_recv[0, 8 * c : 8 * c + 8, :].astype(F32)
+        for j in range(1, segs):
+            total += part_recv[j, 8 * c : 8 * c + 8, :].astype(F32)
+        out[:, c, :] = total * scale[:, c : c + 1]
+
     for o in range(zs):
         for p in range(2):
 
@@ -586,9 +625,9 @@
             pltpu.VMEM((2, chans, 16, 512), BF16),
             pltpu.VMEM((2, chans, 16, 512), BF16),
             pltpu.VMEM((8, chans, 16, 512), BF16),
-            pltpu.VMEM((chans, 512, LAGS), BF16),
-            pltpu.VMEM((256, 512), BF16),
-            pltpu.VMEM((256, 512), BF16),
+            pltpu.VMEM((chans, 768, LAGS), BF16),
+            pltpu.VMEM((512, 768), BF16),
+            pltpu.VMEM((512, 768), BF16),
             pltpu.VMEM((512, LAGS), F32),
             pltpu.VMEM((512, LAGS), BF16),
             pltpu.VMEM((segs, 64, LAGS), BF16),

time: 56.3 us -> 50.6 us (0.90)
  Pallas kernels: 54.2 us -> 48.6 us
    pallas_call x1, Pallas kernels: 54.2 us -> 48.6 us  [local(): pl.pallas_call(body, name='correlate', out_shape=jax.ShapeDtypeStruct((8,...]
where the time goes in v4:
time: 50.6 us; the launch traced here: 50.2 us
  Pallas kernels  48.6 us (96%)
  local copies, waits for them, and re-layouts  1.57 us (3%)
    pallas_call x1, Pallas kernels, local(): pl.pallas_call(body, name='correlate', out_shape=jax.ShapeDtypeStruct((8,...  48.6 us
    unnamed x1, local copies, waits for them, and re-layouts  1.57 us

profile of v4, /device:TPU:1, one launch (start us, length us, event | category | flops | bytes accessed | tf_op | source)
XLA Modules:
  0.0 50.2 jit_solution(10391107665446235365)
XLA Ops:
  0.0 48.6 %correlate.1 = f32[8,8,512]{2,1,0:T(8,128)} custom-call(s32[64]{0:T(128)} %sources.1, f32[4,480,128]{2,1,0:T(8,128)} %bitcast.1, s32[32,128]{1,0:T(8,128)} %validity.1, f32[2,16,512]{2,1,0:T(8,128)} %constant.10.clone.twist_in, bf16[2,512,256]{2,1,0:T(8,128)(2,1)} %constant.11.clone.second_hi, bf16[2,512,256]{2,1,0:T(8,128)(2,1)} %constant.12.clone.second_lo, ...), custom_call_target="tpu_custom_call" | custom-call | tf_op jit(solution)/shard_map/correlate/pallas_call | solution.py:604
  48.6 1.6 %copy.10 = f32[8,8,512]{2,1,0:T(8,128)} copy(f32[8,8,512]{2,1,0:T(8,128)} %correlate.1) | data formatting | bytes 262144

commit v5 on v4

--- a/solution.py
+++ b/solution.py
@@ -116,8 +116,10 @@
     src_send,
     own_recv,
     src_recv,
-    h_hi,
-    h_lo,
+    hi_a,
+    hi_b,
+    lo_a,
+    lo_b,
     table_hi,
     table_lo,
     spec,
@@ -134,10 +136,8 @@
     in_sem,
     own_ss,
     own_rs,
-    src_ss,
-    src_rs,
+    src_sem,
     ag_ss,
-    fw_ss,
     ag_rs,
     wh_ss,
     wh_rs,
@@ -148,10 +148,8 @@
     segs = lax.axis_size("seg")
     me = lax.axis_index("chan")
     seg = lax.axis_index("seg")
-    chip = me // 2
-    core = me % 2
-    z = chip // 2
-    plane = chip % 2
+    chip, core = lax.div(me, 2), lax.rem(me, 2)
+    z, plane = lax.div(chip, 2), lax.rem(chip, 2)
     zs = chans // 4
     block_len = traces.shape[1]
     partner = (2 * chip + 1 - core, seg)
@@ -170,22 +168,22 @@
         )
 
     def device(zz, pp, cc):
-        return (zz % zs) * 4 + pp * 2 + cc
+        return lax.rem(zz, zs) * 4 + pp * 2 + cc
 
     def octet_of(zz, pp):
-        return 2 * zz + (zz + pp) % 2
+        return 2 * zz + lax.rem(zz + pp, 2)
 
     barrier = pltpu.get_barrier_semaphore()
     for d in sorted(range(1, chans), key=lambda d: abs(d - chans // 2)):
         pl.semaphore_signal(
-            barrier, inc=1, device_id=((me + d) % chans, seg), device_id_type=MESH
+            barrier, inc=1, device_id=(lax.rem(me + d, chans), seg), device_id_type=MESH
         )
     for d in range(1, segs):
         for p in range(2):
             pl.semaphore_signal(
                 barrier,
                 inc=1,
-                device_id=(device(z, p, core), (seg + d) % segs),
+                device_id=(device(z, p, core), lax.rem(seg + d, segs)),
                 device_id_type=MESH,
             )
 
@@ -241,30 +239,31 @@
 
     pl.semaphore_wait(barrier, chans - 1 + 2 * (segs - 1))
 
-    src_copies, own_copies = [], [[], []]
+    others = pl.ds(0, chans - 1)
     for d in range(1, chans):
-        to = (me + d) % chans
-        copy = remote(
-            src_send.at[to % 2, octet_of(to // 4, (to // 2) % 2)],
+        to = lax.rem(me + d, chans)
+        remote(
+            src_send.at[lax.rem(to, 2), octet_of(lax.div(to, 4), lax.rem(lax.div(to, 2), 2))],
             src_recv.at[me],
-            src_ss.at[d],
-            src_rs.at[d],
+            src_sem.at[0],
+            src_sem.at[1],
             (to, seg),
-        )
-        copy.start()
-        src_copies.append(copy)
+        ).start()
     for i in range(2):
         for d in range(1, chans):
-            to = (me + d) % chans
-            copy = remote(
-                own_send.at[i, to],
-                own_recv.at[i, me],
-                own_ss.at[i, d],
-                own_rs.at[i, d],
-                (to, seg),
-            )
-            copy.start()
-            own_copies[i].append(copy)
+            to = lax.rem(me + d, chans)
+            remote(
+                own_send.at[i, to], own_recv.at[i, me], own_ss.at[i], own_rs.at[i], (to, seg)
+            ).start()
+
+    def all_sources():
+        ref = src_recv.at[others]
+        return remote(ref, ref, src_sem.at[0], src_sem.at[1], partner)
+
+    def all_own(i):
+        ref = own_recv.at[i, others]
+        return remote(ref, ref, own_ss.at[i], own_rs.at[i], partner)
+
     src_recv[pl.ds(me, 1)] = src_send[core, pl.ds(octet_of(z, plane), 1)]
     for i in range(2):
         own_recv[i, pl.ds(me, 1)] = own_send[i, pl.ds(me, 1)]
@@ -272,14 +271,13 @@
     for n in range(5, 11):
         fetch[n].wait()
 
-    table_hi[:512, :256] = sec_hi[0]
-    table_hi[512:, :256] = sec_hi[1]
-    table_hi[:512, 256:] = -sec_hi[1]
-    table_hi[512:, 256:] = sec_hi[0]
-    table_lo[:512, :256] = sec_lo[0]
-    table_lo[512:, :256] = sec_lo[1]
-    table_lo[:512, 256:] = -sec_lo[1]
-    table_lo[512:, 256:] = sec_lo[0]
+    for table, sec in ((table_hi, sec_hi), (table_lo, sec_lo)):
+        for n in range(2):
+            at, low = slice(256 * n, 256 * n + 256), 512 * n
+            table[low : low + 256, :256] = sec[0, at]
+            table[low : low + 256, 256:] = -sec[1, at]
+            table[low + 256 : low + 512, :256] = sec[1, at]
+            table[low + 256 : low + 512, 256:] = sec[0, at]
 
     def fill(k1, carry):
         c1 = one[0, pl.ds(k1, 1), :]
@@ -338,6 +336,12 @@
 
     spread = (iota((256, 256), 0) // 8 == iota((256, 256), 1) // 8).astype(F32).astype(BF16)
 
+    def half_dot(hi, lo, low):
+        at = slice(low, low + 512)
+        return (
+            dot(hi[...], table_hi[at]) + dot(lo[...], table_hi[at]) + dot(hi[...], table_lo[at])
+        )
+
     def transform(recv, gate, store):
         units = []
         for p in range(chans):
@@ -345,6 +349,7 @@
             at = block_len - 384
             units.append(jnp.exp2(last[:, at : at + 1] * (1.0 / 128.0)) * (1.0 / STEPS))
         for a in range(0, 512, 128):
+            h_hi, h_lo = (hi_a, lo_a) if a < 256 else (hi_b, lo_b)
             xs = [
                 recv[p, :, a : a + 128].astype(jnp.int32).astype(F32) * units[p]
                 for p in range(chans)
@@ -361,16 +366,15 @@
                     re, im = re * c + im * s, im * c - re * s
                 at = slice(16 * k, 16 * k + 16)
                 hi, lo = split(re)
-                h_hi[at, a : a + 128] = hi
-                h_lo[at, a : a + 128] = lo
+                b = a % 256
+                h_hi[at, b : b + 128] = hi
+                h_lo[at, b : b + 128] = lo
                 hi, lo = split(im)
-                h_hi[at, 512 + a : 640 + a] = hi
-                h_lo[at, 512 + a : 640 + a] = lo
-        spec[...] = (
-            dot(h_hi[...], table_hi[...])
-            + dot(h_lo[...], table_hi[...])
-            + dot(h_hi[...], table_lo[...])
-        )
+                h_hi[at, 256 + b : 384 + b] = hi
+                h_lo[at, 256 + b : 384 + b] = lo
+            if a == 128:
+                spec[...] = half_dot(hi_a, lo_a, 0)
+        spec[...] += half_dot(hi_b, lo_b, 512)
         total = None
         for k in range(chans):
             re, im = spec[16 * k : 16 * k + 16, :256], spec[16 * k : 16 * k + 16, 256:]
@@ -392,27 +396,25 @@
     def store_src(k, at, value):
         gathered[slot, k, :, at] = value
 
-    for copy in src_copies:
-        copy.wait_recv()
+    all_sources().wait_recv()
     transform(src_recv, src_gate, store_src)
 
     def gather(ch, d):
         ref = gathered.at[slot, span(ch)]
         to = partner if d == 0 else (device(z + d, plane, core), seg)
-        return remote(ref, ref, ag_ss.at[ch, d], ag_rs.at[ch, slot], to)
+        return remote(ref, ref, ag_ss.at[0], ag_rs.at[ch, int(d == 0)], to)
 
     def slot_of(d, cc):
-        return 2 * ((z + d) % zs) + cc
+        return 2 * lax.rem(z + d, zs) + cc
 
     def forward(ch, d):
         at = slot_of(d, core)
         ref = gathered.at[at, span(ch)]
-        return remote(ref, ref, fw_ss.at[ch, d], ag_rs.at[ch, at], partner)
-
-    def arrive(ch, d, cc):
-        at = slot_of(d, cc)
-        ref = gathered.at[at, span(ch)]
-        remote(ref, ref, fw_ss.at[ch, 0], ag_rs.at[ch, at], partner).wait_recv()
+        return remote(ref, ref, ag_ss.at[1], ag_rs.at[ch, 1], partner)
+
+    def arrive(ch, way, blocks):
+        ref = gathered.at[pl.ds(0, blocks), span(ch)]
+        remote(ref, ref, ag_ss.at[0], ag_rs.at[ch, way], partner).wait_recv()
 
     for ch in range(CHUNKS):
         for d in range(zs - 1, -1, -1):
@@ -427,8 +429,8 @@
         return remote(
             white_send.at[i, span(ch)],
             white_recv.at[i, span(ch)],
-            wh_ss.at[i, ch],
-            wh_rs.at[i, ch],
+            wh_ss.at[0],
+            wh_rs.at[ch],
             across,
         )
 
@@ -438,8 +440,7 @@
             white_send[i, k, :, at] = value
             white[plane, k, 16 * i : 16 * i + 16, at] = value.astype(F32)
 
-        for copy in own_copies[i]:
-            copy.wait_recv()
+        all_own(i).wait_recv()
         transform(own_recv.at[i], own_gates[i], store_own)
         for pair in [(0, ch) for ch in range(3)] if i == 0 else rest:
             cross(*pair).start()
@@ -488,15 +489,15 @@
                         ).astype(BF16)
 
     def relay(ch):
+        arrive(ch, 0, zs - 1)
         for d in range(1, zs):
-            arrive(ch, d, core)
             forward(ch, d).start()
 
     def ready(ch):
-        for d in range(zs):
-            arrive(ch, d, 1 - core)
+        arrive(ch, 1, zs)
+        ref = white_recv.at[:, span(ch)]
+        remote(ref, ref, wh_ss.at[0], wh_rs.at[ch], partner).wait_recv()
         for i in range(2):
-            cross(i, ch).wait_recv()
             for j in range(per):
                 k = ch * per + j
                 white[1 - plane, k, 16 * i : 16 * i + 16, :] = white_recv[i, k].astype(F32)
@@ -559,21 +560,20 @@
     lags(1, last + 1, prod_b)
     scatter(1)
 
-    for copy in src_copies + own_copies[0] + own_copies[1]:
-        copy.wait_send()
-    for ch in range(CHUNKS):
-        for d in range(zs):
-            gather(ch, d).wait_send()
-        for d in range(1, zs):
-            forward(ch, d).wait_send()
-        for i in range(2):
-            cross(i, ch).wait_send()
+    all_sources().wait_send()
+    for i in range(2):
+        all_own(i).wait_send()
+    for n, blocks in enumerate((zs, zs - 1)):
+        ref = gathered.at[pl.ds(0, blocks)]
+        remote(ref, ref, ag_ss.at[n], ag_rs.at[0, 0], partner).wait_send()
+    remote(white_send, white_recv, wh_ss.at[0], wh_rs.at[0], partner).wait_send()
+
     def landed(d):
-        at = (seg + d) % segs
+        at = lax.rem(seg + d, segs)
         ref = part_recv.at[at]
         remote(ref, ref, rs_ss.at[0, 0], rs_rs.at[at], partner).wait_recv()
 
-    @pl.when((seg + seg // 2) % 2 != plane)
+    @pl.when(lax.rem(seg + lax.div(seg, 2), 2) != plane)
     def _():
         landed(0)
 
@@ -616,8 +616,7 @@
             pltpu.VMEM((2, chans // 2, 16, 512), jnp.int16),
             pltpu.VMEM((2, chans, 16, 512), jnp.int16),
             pltpu.VMEM((chans, 16, 512), jnp.int16),
-            pltpu.VMEM((16 * chans, 1024), BF16),
-            pltpu.VMEM((16 * chans, 1024), BF16),
+            *[pltpu.VMEM((16 * chans, 512), BF16)] * 4,
             pltpu.VMEM((1024, 512), BF16),
             pltpu.VMEM((1024, 512), BF16),
             pltpu.VMEM((16 * chans, 512), F32),
@@ -632,15 +631,13 @@
             pltpu.VMEM((512, LAGS), BF16),
             pltpu.VMEM((segs, 64, LAGS), BF16),
             dma((11,)),
-            dma((2, chans)),
-            dma((2, chans)),
-            dma((chans,)),
-            dma((chans,)),
-            dma((CHUNKS, 4)),
-            dma((CHUNKS, 4)),
-            dma((CHUNKS, 8)),
-            dma((2, CHUNKS)),
-            dma((2, CHUNKS)),
+            dma((2,)),
+            dma((2,)),
+            dma((2,)),
+            dma((2,)),
+            dma((CHUNKS, 2)),
+            dma((1,)),
+            dma((CHUNKS,)),
             dma((4, 2)),
             dma((segs,)),
         ],

time: 50.6 us -> 48.4 us (0.957)
  Pallas kernels: 48.6 us -> 46.5 us
    pallas_call x1, Pallas kernels: 48.6 us -> 46.5 us  [local(): pl.pallas_call(body, name='correlate', out_shape=jax.ShapeDtypeStruct((8,...]
where the time goes in v5:
time: 48.4 us; the launch traced here: 48 us
  Pallas kernels  46.5 us (96%)
  local copies, waits for them, and re-layouts  1.57 us (3%)
    pallas_call x1, Pallas kernels, local(): pl.pallas_call(body, name='correlate', out_shape=jax.ShapeDtypeStruct((8,...  46.5 us
    unnamed x1, local copies, waits for them, and re-layouts  1.57 us

profile of v5, /device:TPU:1, one launch (start us, length us, event | category | flops | bytes accessed | tf_op | source)
XLA Modules:
  0.0 48.0 jit_solution(10237545707524774050)
XLA Ops:
  0.0 46.5 %correlate.1 = f32[8,8,512]{2,1,0:T(8,128)} custom-call(s32[64]{0:T(128)} %sources.1, f32[4,480,128]{2,1,0:T(8,128)} %bitcast.1, s32[32,128]{1,0:T(8,128)} %validity.1, f32[2,16,512]{2,1,0:T(8,128)} %constant.10.clone.twist_in, bf16[2,512,256]{2,1,0:T(8,128)(2,1)} %constant.11.clone.second_hi, bf16[2,512,256]{2,1,0:T(8,128)(2,1)} %constant.12.clone.second_lo, ...), custom_call_target="tpu_custom_call" | custom-call | tf_op jit(solution)/shard_map/correlate/pallas_call | solution.py:604
  46.5 1.6 %copy.10 = f32[8,8,512]{2,1,0:T(8,128)} copy(f32[8,8,512]{2,1,0:T(8,128)} %correlate.1) | data formatting | bytes 262144

commit v6 on v5

--- a/solution.py
+++ b/solution.py
@@ -240,8 +240,16 @@
     pl.semaphore_wait(barrier, chans - 1 + 2 * (segs - 1))
 
     others = pl.ds(0, chans - 1)
-    for d in range(1, chans):
-        to = lax.rem(me + d, chans)
+    peers = sorted(
+        [(dz, dx, dc) for dz in range(zs) for dx in range(2) for dc in range(2)][1:],
+        key=lambda t: -(2 * min(t[0], zs - t[0]) + 4 * t[1] + t[2]),
+    )
+
+    def peer(t):
+        return device(z + t[0], lax.rem(plane + t[1], 2), lax.rem(core + t[2], 2))
+
+    for t in peers:
+        to = peer(t)
         remote(
             src_send.at[lax.rem(to, 2), octet_of(lax.div(to, 4), lax.rem(lax.div(to, 2), 2))],
             src_recv.at[me],
@@ -250,8 +258,8 @@
             (to, seg),
         ).start()
     for i in range(2):
-        for d in range(1, chans):
-            to = lax.rem(me + d, chans)
+        for t in peers:
+            to = peer(t)
             remote(
                 own_send.at[i, to], own_recv.at[i, me], own_ss.at[i], own_rs.at[i], (to, seg)
             ).start()
@@ -421,8 +429,8 @@
             gather(ch, d).start()
 
     rest = [(1, ch) for ch in range(CHUNKS)]
-    for ch in range(3, CHUNKS):
-        rest.insert(2 * ch - 3, (0, ch))
+    for ch in range(2, CHUNKS):
+        rest.insert(2 * ch - 2, (0, ch))
     across = (device(z, 1 - plane, core), seg)
 
     def cross(i, ch):
@@ -442,7 +450,7 @@
 
         all_own(i).wait_recv()
         transform(own_recv.at[i], own_gates[i], store_own)
-        for pair in [(0, ch) for ch in range(3)] if i == 0 else rest:
+        for pair in [(0, ch) for ch in range(2)] if i == 0 else rest:
             cross(*pair).start()
 
     acc[...] = jnp.zeros_like(acc)
@@ -505,7 +513,7 @@
     bufs = [prod_a, prod_b]
 
     def chunk(ch, carry):
-        relay(ch + 1)
+        pl.when(ch + 2 < CHUNKS)(lambda: relay(ch + 2))
         ready(ch)
         for j in range(per):
             k = ch * per + j
@@ -515,6 +523,7 @@
         return carry
 
     relay(0)
+    relay(1)
     lax.fori_loop(0, CHUNKS - 1, chunk, 0)
 
     def partial(o, p):

time: 48.4 us -> 46.5 us (0.961)
  Pallas kernels: 46.5 us -> 44.8 us
    pallas_call x1, Pallas kernels: 46.5 us -> 44.8 us  [local(): pl.pallas_call(body, name='correlate', out_shape=jax.ShapeDtypeStruct((8,...]
where the time goes in v6:
time: 46.5 us; the launch traced here: 46.4 us
  Pallas kernels  44.8 us (96%)
  local copies, waits for them, and re-layouts  1.57 us (3%)
    pallas_call x1, Pallas kernels, local(): pl.pallas_call(body, name='correlate', out_shape=jax.ShapeDtypeStruct((8,...  44.8 us
    unnamed x1, local copies, waits for them, and re-layouts  1.57 us

profile of v6, /device:TPU:1, one launch (start us, length us, event | category | flops | bytes accessed | tf_op | source)
XLA Modules:
  0.0 46.4 jit_solution(12699365215375252931)
XLA Ops:
  0.0 44.8 %correlate.1 = f32[8,8,512]{2,1,0:T(8,128)} custom-call(s32[64]{0:T(128)} %sources.1, f32[4,480,128]{2,1,0:T(8,128)} %bitcast.1, s32[32,128]{1,0:T(8,128)} %validity.1, f32[2,16,512]{2,1,0:T(8,128)} %constant.10.clone.twist_in, bf16[2,512,256]{2,1,0:T(8,128)(2,1)} %constant.11.clone.second_hi, bf16[2,512,256]{2,1,0:T(8,128)(2,1)} %constant.12.clone.second_lo, ...), custom_call_target="tpu_custom_call" | custom-call | tf_op jit(solution)/shard_map/correlate/pallas_call | solution.py:613
  44.8 1.6 %copy.10 = f32[8,8,512]{2,1,0:T(8,128)} copy(f32[8,8,512]{2,1,0:T(8,128)} %correlate.1) | data formatting | bytes 262144

commit v7 on v6

--- a/solution.py
+++ b/solution.py
@@ -456,13 +456,16 @@
     acc[...] = jnp.zeros_like(acc)
     prod_b[...] = jnp.zeros_like(prod_b)
 
+    def octet_at(pos):
+        return lax.rem(lax.div(seg, 2) + (2, 1, 3, 0)[pos], zs)
+
     def stack(k, half, prod):
         for l in range(2):
             re_at, im_at = l * 128, 256 + l * 128
             ar, ap, am = [], [], []
             for oo in range(2):
                 for h in range(2):
-                    slot_at = 2 * (2 * half + oo) + h
+                    slot_at = 2 * octet_at(2 * half + oo) + h
                     re = gathered[slot_at, k, :, re_at : re_at + 128].astype(F32)
                     im = gathered[slot_at, k, :, im_at : im_at + 128].astype(F32)
                     for part in (slice(0, 8), slice(8, 16)):
@@ -528,11 +531,11 @@
 
     def partial(o, p):
         rows = part_send.at[128 * o + 64 * p : 128 * o + 64 * p + 64]
-        to = (device(z, p, core), octet_of(o, plane))
+        to = (device(z, p, core), octet_of(octet_at(o), plane))
         return remote(rows, part_recv.at[seg], rs_ss.at[o, p], rs_rs.at[seg], to)
 
     def remains(o, p):
-        return jnp.logical_and(plane == p, seg == octet_of(o, plane))
+        return jnp.logical_and(plane == p, seg == octet_of(octet_at(o), plane))
 
     def scatter(half):
         part_send[256 * half : 256 * half + 256] = acc[256 * half : 256 * half + 256].astype(BF16)

time: 46.5 us -> 46.4 us (level)
  no operation moved by 1% of the time
where the time goes in v7:
time: 46.4 us; the launch traced here: 46.3 us
  Pallas kernels  44.7 us (96%)
  local copies, waits for them, and re-layouts  1.57 us (3%)
    pallas_call x1, Pallas kernels, local(): pl.pallas_call(body, name='correlate', out_shape=jax.ShapeDtypeStruct((8,...  44.7 us
    unnamed x1, local copies, waits for them, and re-layouts  1.57 us

profile of v7, /device:TPU:1, one launch (start us, length us, event | category | flops | bytes accessed | tf_op | source)
XLA Modules:
  0.0 46.3 jit_solution(12987986407155328318)
XLA Ops:
  0.0 44.7 %correlate.1 = f32[8,8,512]{2,1,0:T(8,128)} custom-call(s32[64]{0:T(128)} %sources.1, f32[4,480,128]{2,1,0:T(8,128)} %bitcast.1, s32[32,128]{1,0:T(8,128)} %validity.1, f32[2,16,512]{2,1,0:T(8,128)} %constant.10.clone.twist_in, bf16[2,512,256]{2,1,0:T(8,128)(2,1)} %constant.11.clone.second_hi, bf16[2,512,256]{2,1,0:T(8,128)(2,1)} %constant.12.clone.second_lo, ...), custom_call_target="tpu_custom_call" | custom-call | tf_op jit(solution)/shard_map/correlate/pallas_call | solution.py:616
  44.7 1.6 %copy.10 = f32[8,8,512]{2,1,0:T(8,128)} copy(f32[8,8,512]{2,1,0:T(8,128)} %correlate.1) | data formatting | bytes 262144
